TPU v7x, 1024 devices: a whole 8x8x8 slice. The times are simulated.
1024 devices in a mesh: ctx: 128 (over y, x, core), tp: 8 (over z).
Axes of the slice: x: 8, y: 8, z: 8, core: 2. Of those that a mesh axis runs over, the one named last changes fastest.
Arguments:
- hidden_in: bfloat16 [16384, 4096], P('ctx'), may hold values from -6 to 6
- in_proj: bfloat16 [4096, 3, 2048], P(None, None, 'tp'), may hold values from -1 to 1
- short_taps: bfloat16 [3, 3, 2048], P(None, None, 'tp'), may hold values from -2.5 to 2.5
- long_filters: float32 [16384, 128], P('ctx', 'tp'), may hold values from -2 to 2
- skip_gain: float32 [2048], P('tp'), may hold values from 0.5 to 1.5
- out_proj: bfloat16 [2048, 4096], P(None, 'tp'), may hold values from -1 to 1
Outputs:
- block_out: bfloat16 [16384, 4096], P('ctx', 'tp')
All inputs are finite; a program needn't handle non-finite values.
Results may differ from a plain program's by a relative error of at most 0.015.
Values may be sent and summed in bfloat16 or wider, within the bound.
A program may use at most 64 MiB of HBM per device.

v0:
```python
import jax
import jax.numpy as jnp
from jax import lax
from jax.sharding import PartitionSpec as P

FG = 16
KS = 3


def for_sending(x):

    def short(part):
        return part.astype(jnp.bfloat16) if part.dtype == jnp.float32 else part

    return jax.tree.map(short, x)


def partner(x, axis, stride):
    return lax.ppermute(x, axis, [(i, i ^ 1 << stride) for i in range(lax.axis_size(axis))])


def shifted(x, axis, by):
    count = lax.axis_size(axis)
    pairs = [(i, i + by) for i in range(count) if 0 <= i + by < count]
    return lax.ppermute(x, axis, pairs)


def cmul(a_re, a_im, b_re, b_im):
    return (a_re * b_re - a_im * b_im, a_re * b_im + a_im * b_re)


def dft_tables(count):
    places = jnp.arange(count, dtype=jnp.int32)
    phase = places[:, None] * places[None, :] % count
    angle = 2.0 * jnp.pi / count * phase.astype(jnp.float32)
    return (jnp.cos(angle), jnp.sin(angle))


def apply_table(table, values):
    return jnp.einsum("km,emw->ekw", table, values, precision=lax.Precision.HIGHEST)


def spread(sig_re, sig_im, index, count):
    angle = -jnp.pi * index.astype(jnp.float32) / count
    turn_re, turn_im = cmul(sig_re, sig_im, jnp.cos(angle), jnp.sin(angle))
    return (jnp.stack([sig_re, turn_re]), jnp.stack([sig_im, turn_im]))


def forward_step(self_re, self_im, other_re, other_im, upper, turn_re, turn_im):
    high_re, high_im = cmul(other_re - self_re, other_im - self_im, turn_re, turn_im)
    return (
        jnp.where(upper, high_re, self_re + other_re),
        jnp.where(upper, high_im, self_im + other_im),
    )


def long_conv(sig_re, sig_im, long_filters, repeat):
    count = lax.axis_size("ctx")
    bits = count.bit_length() - 1
    index = lax.axis_index("ctx")
    rows = sig_re.shape[0]
    total = 2 * count * rows
    flipped = jnp.zeros((), jnp.int32)
    for level in range(bits):
        flipped = flipped + (index >> level & 1) * (1 << bits - 1 - level)
    sig_wide = sig_re.shape[1]
    filt_wide = long_filters.shape[1]
    u_re, u_im = spread(sig_re, sig_im, index, count)
    h_re, h_im = spread(long_filters, jnp.zeros_like(long_filters), index, count)
    for level in reversed(range(bits)):
        half = 1 << level
        upper = index >> level & 1 == 1
        angle = -jnp.pi * (index % half).astype(jnp.float32) / half
        turn_re = jnp.cos(angle)
        turn_im = jnp.sin(angle)
        other_u, other_h = partner(
            (
                for_sending(jnp.concatenate([u_re, u_im], -1)),
                for_sending(jnp.concatenate([h_re, h_im], -1)),
            ),
            "ctx",
            level,
        )
        u_re, u_im = forward_step(
            u_re, u_im, other_u[..., :sig_wide], other_u[..., sig_wide:], upper, turn_re, turn_im
        )
        h_re, h_im = forward_step(
            h_re, h_im, other_h[..., :filt_wide], other_h[..., filt_wide:], upper, turn_re, turn_im
        )
    places = jnp.arange(rows, dtype=jnp.int32)[None, :, None]
    branch = jnp.arange(2, dtype=jnp.int32)[:, None, None]
    phase = places * (branch + 2 * flipped) % total
    angle = 2.0 * jnp.pi / total * phase.astype(jnp.float32)
    twist_re = jnp.cos(angle)
    twist_im = jnp.sin(angle)
    cosine, sine = dft_tables(rows)
    u_re, u_im = cmul(u_re, u_im, twist_re, -twist_im)
    h_re, h_im = cmul(h_re, h_im, twist_re, -twist_im)
    spec_u_re = apply_table(cosine, u_re) + apply_table(sine, u_im)
    spec_u_im = apply_table(cosine, u_im) - apply_table(sine, u_re)
    spec_h_re = apply_table(cosine, h_re) + apply_table(sine, h_im)
    spec_h_im = apply_table(cosine, h_im) - apply_table(sine, h_re)
    spec_h_re = jnp.repeat(spec_h_re, repeat, axis=-1)
    spec_h_im = jnp.repeat(spec_h_im, repeat, axis=-1)
    prod_re, prod_im = cmul(spec_u_re, spec_u_im, spec_h_re, spec_h_im)
    back_re = (apply_table(cosine, prod_re) - apply_table(sine, prod_im)) / rows
    back_im = (apply_table(cosine, prod_im) + apply_table(sine, prod_re)) / rows
    back_re, back_im = cmul(back_re, back_im, twist_re, twist_im)
    for level in range(bits):
        half = 1 << level
        upper = index >> level & 1 == 1
        angle = jnp.pi * (index % half).astype(jnp.float32) / half
        turn_re = jnp.cos(angle)
        turn_im = jnp.sin(angle)
        other = partner(for_sending(jnp.concatenate([back_re, back_im], -1)), "ctx", level)
        other_re = other[..., :sig_wide]
        other_im = other[..., sig_wide:]
        lower_re, lower_im = cmul(other_re, other_im, turn_re, turn_im)
        upper_re, upper_im = cmul(back_re, back_im, turn_re, turn_im)
        back_re = jnp.where(upper, other_re - upper_re, back_re + lower_re) * 0.5
        back_im = jnp.where(upper, other_im - upper_im, back_im + lower_im) * 0.5
    angle = jnp.pi * index.astype(jnp.float32) / count
    last_re, last_im = cmul(back_re[1], back_im[1], jnp.cos(angle), jnp.sin(angle))
    return ((back_re[0] + last_re) * 0.5, (back_im[0] + last_im) * 0.5)


def per_device(hidden_in, in_proj, short_taps, long_filters, skip_gain, out_proj):
    rows, model = hidden_in.shape
    width = in_proj.shape[2]
    proj = jnp.dot(hidden_in, in_proj.reshape(model, 3 * width), preferred_element_type=jnp.float32)
    proj = lax.optimization_barrier(proj.astype(jnp.bfloat16)).reshape(rows, 3, width)
    previous = shifted(proj[rows - (KS - 1) :], "ctx", 1)
    extended = jnp.concatenate([previous, proj], 0)
    feat = jnp.zeros((rows, 3, width), jnp.float32)
    for shift_back in range(KS):
        start = KS - 1 - shift_back
        feat = feat + short_taps[shift_back].astype(jnp.float32)[None] * extended[
            start : start + rows
        ].astype(jnp.float32)
    query = feat[:, 0, :]
    gated = feat[:, 1, :] * feat[:, 2, :]
    conv_re, conv_im = long_conv(gated, jnp.zeros_like(gated), long_filters, FG)
    hidden = (query * (conv_re + skip_gain[None, :] * gated)).astype(jnp.bfloat16)
    summed = jnp.dot(
        lax.all_gather(hidden, "tp", axis=1, tiled=True),
        out_proj,
        preferred_element_type=jnp.float32,
    )
    return summed.astype(jnp.bfloat16)


def solution(mesh):
    in_specs = (
        P("ctx", None),
        P(None, None, "tp"),
        P(None, None, "tp"),
        P("ctx", "tp"),
        P("tp"),
        P(None, "tp"),
    )
    out_specs = P("ctx", "tp")
    return jax.shard_map(
        per_device, mesh=mesh, in_specs=in_specs, out_specs=out_specs, check_vma=False
    )
```

profile of v0, /device:TPU:14, one launch (start us, length us, event | category | flops | bytes accessed | tf_op | source)
XLA Modules:
  0.0 272.3 jit_solution(4168309036697795892)
XLA Ops:
  0.0 8.8 %copy.10 = bf16[4096,3,256]{0,2,1:T(8,128)(2,1)} copy(bf16[4096,3,256]{2,0,1:T(8,128)(2,1)} %param.7) | data formatting | bytes 12582912 | tf_op args[1]
  8.8 5.0 %convolution_convert_fusion = bf16[128,768]{1,0:T(8,128)(2,1)S(1)} fusion(bf16[128,4096]{1,0:T(8,128)(2,1)S(1)} %copy-done.1, bf16[4096,768]{0,1:T(8,128)(2,1)} %bitcast.117), kind=kOutput, calls=%fused_computation | convolution fusion | flops 805404672 | bytes 7536640 | tf_op jit(solution)/shard_map/dot_general | solution.py:130
  16.2 8.2 %collective-permute-start.8 = (bf16[2,128,32]{1,2,0:T(8,128)(2,1)S(1)}, bf16[2,128,32]{1,2,0:T(8,128)(2,1)S(1)}, u32[]{:S(2)}, u32[]{:S(2)}) collective-permute-start(bf16[2,128,32]{1,2,0:T(8,128)(2,1)S(1)} %pad_maximum_fusion.17), channel_id=1, source_target_pairs={{0,512},{8,520},{16,528},{24,536},{32,544},{40,552},{48,560},{56,5... | collective-permute-start | bytes 49160 | tf_op jit(solution)/shard_map/ppermute | solution.py:19
  26.8 3.9 %collective-permute-start.9 = (bf16[2,128,32]{1,2,0:T(8,128)(2,1)S(1)}, bf16[2,128,32]{1,2,0:T(8,128)(2,1)S(1)}, u32[]{:S(2)}, u32[]{:S(2)}) collective-permute-start(bf16[2,128,32]{1,2,0:T(8,128)(2,1)S(1)} %pad_maximum_fusion.18), channel_id=1, source_target_pairs={{0,256},{8,264},{16,272},{24,280},{32,288},{40,296},{48,304},{56,3... | collective-permute-start | bytes 49160 | tf_op jit(solution)/shard_map/ppermute | solution.py:19
  30.8 2.6 collective-permute-done.9
  33.4 2.7 collective-permute-start.10
  36.1 7.2 %collective-permute-start.1 = (bf16[2,128,512]{1,2,0:T(8,128)(2,1)S(1)}, bf16[2,128,512]{1,2,0:T(8,128)(2,1)S(1)}, u32[]{:S(2)}, u32[]{:S(2)}) collective-permute-start(bf16[2,128,512]{1,2,0:T(8,128)(2,1)S(1)} %pad_maximum_fusion.1), channel_id=1, source_target_pairs={{0,512},{8,520},{16,528},{24,536},{32,544},{40,552},{48,560},{56,5... | collective-permute-start | bytes 786440 | tf_op jit(solution)/shard_map/ppermute | solution.py:19
  43.4 5.0 %collective-permute-start.11 = (bf16[2,128,32]{1,2,0:T(8,128)(2,1)S(1)}, bf16[2,128,32]{1,2,0:T(8,128)(2,1)S(1)}, u32[]{:S(2)}, u32[]{:S(2)}) collective-permute-start(bf16[2,128,32]{1,2,0:T(8,128)(2,1)S(1)} %pad_maximum_fusion.20), channel_id=1, source_target_pairs={{0,64},{8,72},{16,80},{24,88},{32,96},{40,104},{48,112},{56,120},{... | collective-permute-start | bytes 49160 | tf_op jit(solution)/shard_map/ppermute | solution.py:19
  48.3 4.9 %collective-permute-done.1 = bf16[2,128,512]{1,2,0:T(8,128)(2,1)S(1)} collective-permute-done((bf16[2,128,512]{1,2,0:T(8,128)(2,1)S(1)}, bf16[2,128,512]{1,2,0:T(8,128)(2,1)S(1)}, u32[]{:S(2)}, u32[]{:S(2)}) %collective-permute-start.1) | collective-permute-done | bytes 262176 | tf_op jit(solution)/shard_map/ppermute | solution.py:19
  53.4 7.0 %collective-permute-start.2 = (bf16[2,128,512]{1,2,0:T(8,128)(2,1)S(1)}, bf16[2,128,512]{1,2,0:T(8,128)(2,1)S(1)}, u32[]{:S(2)}, u32[]{:S(2)}) collective-permute-start(bf16[2,128,512]{1,2,0:T(8,128)(2,1)S(1)} %pad_maximum_fusion.2), channel_id=1, source_target_pairs={{0,256},{8,264},{16,272},{24,280},{32,288},{40,296},{48,304},{56,3... | collective-permute-start | bytes 786440 | tf_op jit(solution)/shard_map/ppermute | solution.py:19
  60.5 2.5 collective-permute-start.12
  63.0 6.7 %collective-permute-done.2 = bf16[2,128,512]{1,2,0:T(8,128)(2,1)S(1)} collective-permute-done((bf16[2,128,512]{1,2,0:T(8,128)(2,1)S(1)}, bf16[2,128,512]{1,2,0:T(8,128)(2,1)S(1)}, u32[]{:S(2)}, u32[]{:S(2)}) %collective-permute-start.2) | collective-permute-done | bytes 262176 | tf_op jit(solution)/shard_map/ppermute | solution.py:19
  69.9 2.6 collective-permute-start.3
  72.6 3.1 %collective-permute-start.13 = (bf16[2,128,32]{1,2,0:T(8,128)(2,1)S(1)}, bf16[2,128,32]{1,2,0:T(8,128)(2,1)S(1)}, u32[]{:S(2)}, u32[]{:S(2)}) collective-permute-start(bf16[2,128,32]{1,2,0:T(8,128)(2,1)S(1)} %pad_maximum_fusion.22), channel_id=1, source_target_pairs={{0,16},{8,24},{16,0},{24,8},{32,48},{40,56},{48,32},{56,40},{64,80... | collective-permute-start | bytes 49160 | tf_op jit(solution)/shard_map/ppermute | solution.py:19
  75.7 3.8 %collective-permute-done.3 = bf16[2,128,512]{1,2,0:T(8,128)(2,1)S(1)} collective-permute-done((bf16[2,128,512]{1,2,0:T(8,128)(2,1)S(1)}, bf16[2,128,512]{1,2,0:T(8,128)(2,1)S(1)}, u32[]{:S(2)}, u32[]{:S(2)}) %collective-permute-start.3) | collective-permute-done | bytes 262176 | tf_op jit(solution)/shard_map/ppermute | solution.py:19
  79.7 7.5 %collective-permute-start.4 = (bf16[2,128,512]{1,2,0:T(8,128)(2,1)S(1)}, bf16[2,128,512]{1,2,0:T(8,128)(2,1)S(1)}, u32[]{:S(2)}, u32[]{:S(2)}) collective-permute-start(bf16[2,128,512]{1,2,0:T(8,128)(2,1)S(1)} %pad_maximum_fusion.4), channel_id=1, source_target_pairs={{0,64},{8,72},{16,80},{24,88},{32,96},{40,104},{48,112},{56,120},{... | collective-permute-start | bytes 786440 | tf_op jit(solution)/shard_map/ppermute | solution.py:19
  90.3 7.5 %collective-permute-done.4 = bf16[2,128,512]{1,2,0:T(8,128)(2,1)S(1)} collective-permute-done((bf16[2,128,512]{1,2,0:T(8,128)(2,1)S(1)}, bf16[2,128,512]{1,2,0:T(8,128)(2,1)S(1)}, u32[]{:S(2)}, u32[]{:S(2)}) %collective-permute-start.4) | collective-permute-done | bytes 262176 | tf_op jit(solution)/shard_map/ppermute | solution.py:19
  101.4 9.5 %collective-permute-done.5 = bf16[2,128,512]{1,2,0:T(8,128)(2,1)S(1)} collective-permute-done((bf16[2,128,512]{1,2,0:T(8,128)(2,1)S(1)}, bf16[2,128,512]{1,2,0:T(8,128)(2,1)S(1)}, u32[]{:S(2)}, u32[]{:S(2)}) %collective-permute-start.5) | collective-permute-done | bytes 262176 | tf_op jit(solution)/shard_map/ppermute | solution.py:19
  115.4 4.5 %collective-permute-done.6 = bf16[2,128,512]{1,2,0:T(8,128)(2,1)S(1)} collective-permute-done((bf16[2,128,512]{1,2,0:T(8,128)(2,1)S(1)}, bf16[2,128,512]{1,2,0:T(8,128)(2,1)S(1)}, u32[]{:S(2)}, u32[]{:S(2)}) %collective-permute-start.6) | collective-permute-done | bytes 262176 | tf_op jit(solution)/shard_map/ppermute | solution.py:19
  129.7 2.4 collective-permute-start.15
  133.5 2.2 collective-permute-start.16
  135.9 8.1 %collective-permute-done.16 = bf16[2,128,512]{1,2,0:T(8,128)(2,1)S(1)} collective-permute-done((bf16[2,128,512]{1,2,0:T(8,128)(2,1)S(1)}, bf16[2,128,512]{1,2,0:T(8,128)(2,1)S(1)}, u32[]{:S(2)}, u32[]{:S(2)}) %collective-permute-start.16) | collective-permute-done | bytes 262176 | tf_op jit(solution)/shard_map/ppermute | solution.py:19
  148.0 13.8 %collective-permute-done.17 = bf16[2,128,512]{1,2,0:T(8,128)(2,1)S(1)} collective-permute-done((bf16[2,128,512]{1,2,0:T(8,128)(2,1)S(1)}, bf16[2,128,512]{1,2,0:T(8,128)(2,1)S(1)}, u32[]{:S(2)}, u32[]{:S(2)}) %collective-permute-start.17) | collective-permute-done | bytes 262176 | tf_op jit(solution)/shard_map/ppermute | solution.py:19
  163.7 7.0 %collective-permute-start.18 = (bf16[2,128,512]{1,2,0:T(8,128)(2,1)S(1)}, bf16[2,128,512]{1,2,0:T(8,128)(2,1)S(1)}, u32[]{:S(2)}, u32[]{:S(2)}) collective-permute-start(bf16[2,128,512]{1,2,0:T(8,128)(2,1)S(1)} %pad_maximum_fusion.11), channel_id=1, source_target_pairs={{0,64},{8,72},{16,80},{24,88},{32,96},{40,104},{48,112},{56,120},{... | collective-permute-start | bytes 786440 | tf_op jit(solution)/shard_map/ppermute | solution.py:19
  170.9 12.5 %collective-permute-done.18 = bf16[2,128,512]{1,2,0:T(8,128)(2,1)S(1)} collective-permute-done((bf16[2,128,512]{1,2,0:T(8,128)(2,1)S(1)}, bf16[2,128,512]{1,2,0:T(8,128)(2,1)S(1)}, u32[]{:S(2)}, u32[]{:S(2)}) %collective-permute-start.18) | collective-permute-done | bytes 262176 | tf_op jit(solution)/shard_map/ppermute | solution.py:19
  185.4 2.1 collective-permute-start.19
  187.7 6.9 %collective-permute-done.19 = bf16[2,128,512]{1,2,0:T(8,128)(2,1)S(1)} collective-permute-done((bf16[2,128,512]{1,2,0:T(8,128)(2,1)S(1)}, bf16[2,128,512]{1,2,0:T(8,128)(2,1)S(1)}, u32[]{:S(2)}, u32[]{:S(2)}) %collective-permute-start.19) | collective-permute-done | bytes 262176 | tf_op jit(solution)/shard_map/ppermute | solution.py:19
  196.5 4.3 %collective-permute-start.20 = (bf16[2,128,512]{1,2,0:T(8,128)(2,1)S(1)}, bf16[2,128,512]{1,2,0:T(8,128)(2,1)S(1)}, u32[]{:S(2)}, u32[]{:S(2)}) collective-permute-start(bf16[2,128,512]{1,2,0:T(8,128)(2,1)S(1)} %pad_maximum_fusion.13), channel_id=1, source_target_pairs={{0,256},{8,264},{16,272},{24,280},{32,288},{40,296},{48,304},{56,3... | collective-permute-start | bytes 786440 | tf_op jit(solution)/shard_map/ppermute | solution.py:19
  200.9 10.4 %collective-permute-done.20 = bf16[2,128,512]{1,2,0:T(8,128)(2,1)S(1)} collective-permute-done((bf16[2,128,512]{1,2,0:T(8,128)(2,1)S(1)}, bf16[2,128,512]{1,2,0:T(8,128)(2,1)S(1)}, u32[]{:S(2)}, u32[]{:S(2)}) %collective-permute-start.20) | collective-permute-done | bytes 262176 | tf_op jit(solution)/shard_map/ppermute | solution.py:19
  213.3 7.6 %collective-permute-start.21 = (bf16[2,128,512]{1,2,0:T(8,128)(2,1)S(1)}, bf16[2,128,512]{1,2,0:T(8,128)(2,1)S(1)}, u32[]{:S(2)}, u32[]{:S(2)}) collective-permute-start(bf16[2,128,512]{1,2,0:T(8,128)(2,1)S(1)} %pad_maximum_fusion.14), channel_id=1, source_target_pairs={{0,512},{8,520},{16,528},{24,536},{32,544},{40,552},{48,560},{56,5... | collective-permute-start | bytes 786440 | tf_op jit(solution)/shard_map/ppermute | solution.py:19
  221.2 11.3 %collective-permute-done.21 = bf16[2,128,512]{1,2,0:T(8,128)(2,1)S(1)} collective-permute-done((bf16[2,128,512]{1,2,0:T(8,128)(2,1)S(1)}, bf16[2,128,512]{1,2,0:T(8,128)(2,1)S(1)}, u32[]{:S(2)}, u32[]{:S(2)}) %collective-permute-start.21) | collective-permute-done | bytes 262176 | tf_op jit(solution)/shard_map/ppermute | solution.py:19
  232.8 38.4 %all_gather.3 = bf16[128,2048]{0,1:T(8,128)(2,1)S(1)} all-gather(bf16[128,256]{0,1:T(8,128)(2,1)S(1)} %fusion.66), channel_id=1, replica_groups=mesh['ctx'=128,'tp'=8] {'tp'}, dimensions={1}, use_global_device_ids=true | all-gather | bytes 589824 | tf_op jit(solution)/shard_map/all_gather | solution.py:145
  (114 shorter events, 39.0 us)
Async XLA Ops:
  0.0 271.1 %copy-start = (bf16[2048,512]{1,0:T(8,128)(2,1)S(1)}, bf16[2048,512]{1,0:T(8,128)(2,1)}, u32[]{:S(2)}) copy-start(bf16[2048,512]{1,0:T(8,128)(2,1)} %param.11) | copy-start | bytes 6291460
  0.0 8.8 %copy-start.1 = (bf16[128,4096]{1,0:T(8,128)(2,1)S(1)}, bf16[128,4096]{1,0:T(8,128)(2,1)}, u32[]{:S(2)}) copy-start(bf16[128,4096]{1,0:T(8,128)(2,1)} %param.6) | copy-start | bytes 3145732
  8.8 7.3 %copy-start.7 = (f32[128,16]{0,1:T(8,128)S(1)}, f32[128,16]{0,1:T(8,128)}, u32[]{:S(2)}) copy-start(f32[128,16]{0,1:T(8,128)} %param.9) | copy-start | bytes 24580
  8.8 15.9 %copy-start.10 = (bf16[3,3,256]{2,1,0:T(4,128)(2,1)S(1)}, bf16[3,3,256]{2,1,0:T(4,128)(2,1)}, u32[]{:S(2)}) copy-start(bf16[3,3,256]{2,1,0:T(4,128)(2,1)} %param.8) | copy-start | bytes 13828
  14.0 12.2 %collective-permute-start = (bf16[2,3,256]{0,2,1:T(8,128)(2,1)S(1)}, bf16[2,3,256]{0,2,1:T(8,128)(2,1)S(1)}, u32[]{:S(2)}, u32[]{:S(2)}) collective-permute-start(bf16[2,3,256]{0,2,1:T(8,128)(2,1)S(1)} %bitcast.119), channel_id=1, source_target_pairs={{0,8},{8,16},{16,24},{24,32},{32,40},{40,48},{48,56},{56,64},{64,7... | collective-permute-start | bytes 9224 | tf_op jit(solution)/shard_map/ppermute | solution.py:25
  16.2 10.6 %collective-permute-start.8 = (bf16[2,128,32]{1,2,0:T(8,128)(2,1)S(1)}, bf16[2,128,32]{1,2,0:T(8,128)(2,1)S(1)}, u32[]{:S(2)}, u32[]{:S(2)}) collective-permute-start(bf16[2,128,32]{1,2,0:T(8,128)(2,1)S(1)} %pad_maximum_fusion.17), channel_id=1, source_target_pairs={{0,512},{8,520},{16,528},{24,536},{32,544},{40,552},{48,560},{56,5... | collective-permute-start | bytes 49160 | tf_op jit(solution)/shard_map/ppermute | solution.py:19
  26.2 73.8 %copy-start.14 = (s32[2]{0:T(128)S(1)}, s32[2]{0:T(128)}, u32[]{:S(2)}) copy-start(s32[2]{0:T(128)} %iota_add_fusion) | copy-start | bytes 28
  26.8 6.5 %collective-permute-start.9 = (bf16[2,128,32]{1,2,0:T(8,128)(2,1)S(1)}, bf16[2,128,32]{1,2,0:T(8,128)(2,1)S(1)}, u32[]{:S(2)}, u32[]{:S(2)}) collective-permute-start(bf16[2,128,32]{1,2,0:T(8,128)(2,1)S(1)} %pad_maximum_fusion.18), channel_id=1, source_target_pairs={{0,256},{8,264},{16,272},{24,280},{32,288},{40,296},{48,304},{56,3... | collective-permute-start | bytes 49160 | tf_op jit(solution)/shard_map/ppermute | solution.py:19
  33.4 9.9 %collective-permute-start.10 = (bf16[2,128,32]{1,2,0:T(8,128)(2,1)S(1)}, bf16[2,128,32]{1,2,0:T(8,128)(2,1)S(1)}, u32[]{:S(2)}, u32[]{:S(2)}) collective-permute-start(bf16[2,128,32]{1,2,0:T(8,128)(2,1)S(1)} %pad_maximum_fusion.19), channel_id=1, source_target_pairs={{0,128},{8,136},{16,144},{24,152},{32,160},{40,168},{48,176},{56,1... | collective-permute-start | bytes 49160 | tf_op jit(solution)/shard_map/ppermute | solution.py:19
  36.1 17.1 %collective-permute-start.1 = (bf16[2,128,512]{1,2,0:T(8,128)(2,1)S(1)}, bf16[2,128,512]{1,2,0:T(8,128)(2,1)S(1)}, u32[]{:S(2)}, u32[]{:S(2)}) collective-permute-start(bf16[2,128,512]{1,2,0:T(8,128)(2,1)S(1)} %pad_maximum_fusion.1), channel_id=1, source_target_pairs={{0,512},{8,520},{16,528},{24,536},{32,544},{40,552},{48,560},{56,5... | collective-permute-start | bytes 786440 | tf_op jit(solution)/shard_map/ppermute | solution.py:19
  43.4 17.0 %collective-permute-start.11 = (bf16[2,128,32]{1,2,0:T(8,128)(2,1)S(1)}, bf16[2,128,32]{1,2,0:T(8,128)(2,1)S(1)}, u32[]{:S(2)}, u32[]{:S(2)}) collective-permute-start(bf16[2,128,32]{1,2,0:T(8,128)(2,1)S(1)} %pad_maximum_fusion.20), channel_id=1, source_target_pairs={{0,64},{8,72},{16,80},{24,88},{32,96},{40,104},{48,112},{56,120},{... | collective-permute-start | bytes 49160 | tf_op jit(solution)/shard_map/ppermute | solution.py:19
  53.4 16.3 %collective-permute-start.2 = (bf16[2,128,512]{1,2,0:T(8,128)(2,1)S(1)}, bf16[2,128,512]{1,2,0:T(8,128)(2,1)S(1)}, u32[]{:S(2)}, u32[]{:S(2)}) collective-permute-start(bf16[2,128,512]{1,2,0:T(8,128)(2,1)S(1)} %pad_maximum_fusion.2), channel_id=1, source_target_pairs={{0,256},{8,264},{16,272},{24,280},{32,288},{40,296},{48,304},{56,3... | collective-permute-start | bytes 786440 | tf_op jit(solution)/shard_map/ppermute | solution.py:19
  60.5 12.1 %collective-permute-start.12 = (bf16[2,128,32]{1,2,0:T(8,128)(2,1)S(1)}, bf16[2,128,32]{1,2,0:T(8,128)(2,1)S(1)}, u32[]{:S(2)}, u32[]{:S(2)}) collective-permute-start(bf16[2,128,32]{1,2,0:T(8,128)(2,1)S(1)} %pad_maximum_fusion.21), channel_id=1, source_target_pairs={{0,32},{8,40},{16,48},{24,56},{32,0},{40,8},{48,16},{56,24},{64,96... | collective-permute-start | bytes 49160 | tf_op jit(solution)/shard_map/ppermute | solution.py:19
  69.9 9.6 %collective-permute-start.3 = (bf16[2,128,512]{1,2,0:T(8,128)(2,1)S(1)}, bf16[2,128,512]{1,2,0:T(8,128)(2,1)S(1)}, u32[]{:S(2)}, u32[]{:S(2)}) collective-permute-start(bf16[2,128,512]{1,2,0:T(8,128)(2,1)S(1)} %pad_maximum_fusion.3), channel_id=1, source_target_pairs={{0,128},{8,136},{16,144},{24,152},{32,160},{40,168},{48,176},{56,1... | collective-permute-start | bytes 786440 | tf_op jit(solution)/shard_map/ppermute | solution.py:19
  72.6 14.6 %collective-permute-start.13 = (bf16[2,128,32]{1,2,0:T(8,128)(2,1)S(1)}, bf16[2,128,32]{1,2,0:T(8,128)(2,1)S(1)}, u32[]{:S(2)}, u32[]{:S(2)}) collective-permute-start(bf16[2,128,32]{1,2,0:T(8,128)(2,1)S(1)} %pad_maximum_fusion.22), channel_id=1, source_target_pairs={{0,16},{8,24},{16,0},{24,8},{32,48},{40,56},{48,32},{56,40},{64,80... | collective-permute-start | bytes 49160 | tf_op jit(solution)/shard_map/ppermute | solution.py:19
  79.7 18.2 %collective-permute-start.4 = (bf16[2,128,512]{1,2,0:T(8,128)(2,1)S(1)}, bf16[2,128,512]{1,2,0:T(8,128)(2,1)S(1)}, u32[]{:S(2)}, u32[]{:S(2)}) collective-permute-start(bf16[2,128,512]{1,2,0:T(8,128)(2,1)S(1)} %pad_maximum_fusion.4), channel_id=1, source_target_pairs={{0,64},{8,72},{16,80},{24,88},{32,96},{40,104},{48,112},{56,120},{... | collective-permute-start | bytes 786440 | tf_op jit(solution)/shard_map/ppermute | solution.py:19
  88.4 12.3 %collective-permute-start.14 = (bf16[2,128,32]{1,2,0:T(8,128)(2,1)}, bf16[2,128,32]{1,2,0:T(8,128)(2,1)}, u32[]{:S(2)}, u32[]{:S(2)}) collective-permute-start(bf16[2,128,32]{1,2,0:T(8,128)(2,1)} %pad_maximum_fusion.23), channel_id=1, source_target_pairs={{0,8},{8,0},{16,24},{24,16},{32,40},{40,32},{48,56},{56,48},{64,72... | collective-permute-start | bytes 49160 | tf_op jit(solution)/shard_map/ppermute | solution.py:19
  98.0 13.0 %collective-permute-start.5 = (bf16[2,128,512]{1,2,0:T(8,128)(2,1)S(1)}, bf16[2,128,512]{1,2,0:T(8,128)(2,1)S(1)}, u32[]{:S(2)}, u32[]{:S(2)}) collective-permute-start(bf16[2,128,512]{1,2,0:T(8,128)(2,1)S(1)} %pad_maximum_fusion.5), channel_id=1, source_target_pairs={{0,32},{8,40},{16,48},{24,56},{32,0},{40,8},{48,16},{56,24},{64,96... | collective-permute-start | bytes 786440 | tf_op jit(solution)/shard_map/ppermute | solution.py:19
  100.7 23.9 %copy-start.8 = (f32[2,128]{1,0:T(2,128)S(1)}, f32[2,128]{1,0:T(2,128)}, u32[]{:S(2)}) copy-start(f32[2,128]{1,0:T(2,128)} %get-tuple-element.138) | copy-start | bytes 3076
  100.7 23.9 %copy-start.9 = (f32[2,128]{1,0:T(2,128)S(1)}, f32[2,128]{1,0:T(2,128)}, u32[]{:S(2)}) copy-start(f32[2,128]{1,0:T(2,128)} %get-tuple-element.139) | copy-start | bytes 3076
  111.0 18.0 %copy-start.11 = (f32[2,128]{1,0:T(2,128)S(1)}, f32[2,128]{1,0:T(2,128)}, u32[]{:S(2)}) copy-start(f32[2,128]{1,0:T(2,128)} %get-tuple-element.136) | copy-start | bytes 3076
  111.0 18.0 %copy-start.12 = (f32[2,128]{1,0:T(2,128)S(1)}, f32[2,128]{1,0:T(2,128)}, u32[]{:S(2)}) copy-start(f32[2,128]{1,0:T(2,128)} %get-tuple-element.137) | copy-start | bytes 3076
  111.2 8.7 %collective-permute-start.6 = (bf16[2,128,512]{1,2,0:T(8,128)(2,1)S(1)}, bf16[2,128,512]{1,2,0:T(8,128)(2,1)S(1)}, u32[]{:S(2)}, u32[]{:S(2)}) collective-permute-start(bf16[2,128,512]{1,2,0:T(8,128)(2,1)S(1)} %pad_maximum_fusion.6), channel_id=1, source_target_pairs={{0,16},{8,24},{16,0},{24,8},{32,48},{40,56},{48,32},{56,40},{64,80... | collective-permute-start | bytes 786440 | tf_op jit(solution)/shard_map/ppermute | solution.py:19
  120.1 4.4 %collective-permute-start.7 = (bf16[2,128,512]{1,2,0:T(8,128)(2,1)S(1)}, bf16[2,128,512]{1,2,0:T(8,128)(2,1)S(1)}, u32[]{:S(2)}, u32[]{:S(2)}) collective-permute-start(bf16[2,128,512]{1,2,0:T(8,128)(2,1)S(1)} %pad_maximum_fusion.7), channel_id=1, source_target_pairs={{0,8},{8,0},{16,24},{24,16},{32,40},{40,32},{48,56},{56,48},{64,72... | collective-permute-start | bytes 786440 | tf_op jit(solution)/shard_map/ppermute | solution.py:19
  129.7 3.6 %collective-permute-start.15 = (bf16[2,128,512]{1,2,0:T(8,128)(2,1)S(1)}, bf16[2,128,512]{1,2,0:T(8,128)(2,1)S(1)}, u32[]{:S(2)}, u32[]{:S(2)}) collective-permute-start(bf16[2,128,512]{1,2,0:T(8,128)(2,1)S(1)} %pad_maximum_fusion.8), channel_id=1, source_target_pairs={{0,8},{8,0},{16,24},{24,16},{32,40},{40,32},{48,56},{56,48},{64,72... | collective-permute-start | bytes 786440 | tf_op jit(solution)/shard_map/ppermute | solution.py:19
  133.5 10.5 %collective-permute-start.16 = (bf16[2,128,512]{1,2,0:T(8,128)(2,1)S(1)}, bf16[2,128,512]{1,2,0:T(8,128)(2,1)S(1)}, u32[]{:S(2)}, u32[]{:S(2)}) collective-permute-start(bf16[2,128,512]{1,2,0:T(8,128)(2,1)S(1)} %pad_maximum_fusion.9), channel_id=1, source_target_pairs={{0,16},{8,24},{16,0},{24,8},{32,48},{40,56},{48,32},{56,40},{64,80... | collective-permute-start | bytes 786440 | tf_op jit(solution)/shard_map/ppermute | solution.py:19
  144.7 88.0 %copy-start.13 = (f32[256]{0:T(256)S(1)}, f32[256]{0:T(256)}, u32[]{:S(2)}) copy-start(f32[256]{0:T(256)} %param.10) | copy-start | bytes 3076
  145.9 15.9 %collective-permute-start.17 = (bf16[2,128,512]{1,2,0:T(8,128)(2,1)S(1)}, bf16[2,128,512]{1,2,0:T(8,128)(2,1)S(1)}, u32[]{:S(2)}, u32[]{:S(2)}) collective-permute-start(bf16[2,128,512]{1,2,0:T(8,128)(2,1)S(1)} %pad_maximum_fusion.10), channel_id=1, source_target_pairs={{0,32},{8,40},{16,48},{24,56},{32,0},{40,8},{48,16},{56,24},{64,96... | collective-permute-start | bytes 786440 | tf_op jit(solution)/shard_map/ppermute | solution.py:19
  163.7 19.7 %collective-permute-start.18 = (bf16[2,128,512]{1,2,0:T(8,128)(2,1)S(1)}, bf16[2,128,512]{1,2,0:T(8,128)(2,1)S(1)}, u32[]{:S(2)}, u32[]{:S(2)}) collective-permute-start(bf16[2,128,512]{1,2,0:T(8,128)(2,1)S(1)} %pad_maximum_fusion.11), channel_id=1, source_target_pairs={{0,64},{8,72},{16,80},{24,88},{32,96},{40,104},{48,112},{56,120},{... | collective-permute-start | bytes 786440 | tf_op jit(solution)/shard_map/ppermute | solution.py:19
  185.4 9.2 %collective-permute-start.19 = (bf16[2,128,512]{1,2,0:T(8,128)(2,1)S(1)}, bf16[2,128,512]{1,2,0:T(8,128)(2,1)S(1)}, u32[]{:S(2)}, u32[]{:S(2)}) collective-permute-start(bf16[2,128,512]{1,2,0:T(8,128)(2,1)S(1)} %pad_maximum_fusion.12), channel_id=1, source_target_pairs={{0,128},{8,136},{16,144},{24,152},{32,160},{40,168},{48,176},{56,1... | collective-permute-start | bytes 786440 | tf_op jit(solution)/shard_map/ppermute | solution.py:19
  196.5 14.8 %collective-permute-start.20 = (bf16[2,128,512]{1,2,0:T(8,128)(2,1)S(1)}, bf16[2,128,512]{1,2,0:T(8,128)(2,1)S(1)}, u32[]{:S(2)}, u32[]{:S(2)}) collective-permute-start(bf16[2,128,512]{1,2,0:T(8,128)(2,1)S(1)} %pad_maximum_fusion.13), channel_id=1, source_target_pairs={{0,256},{8,264},{16,272},{24,280},{32,288},{40,296},{48,304},{56,3... | collective-permute-start | bytes 786440 | tf_op jit(solution)/shard_map/ppermute | solution.py:19
  213.3 19.2 %collective-permute-start.21 = (bf16[2,128,512]{1,2,0:T(8,128)(2,1)S(1)}, bf16[2,128,512]{1,2,0:T(8,128)(2,1)S(1)}, u32[]{:S(2)}, u32[]{:S(2)}) collective-permute-start(bf16[2,128,512]{1,2,0:T(8,128)(2,1)S(1)} %pad_maximum_fusion.14), channel_id=1, source_target_pairs={{0,512},{8,520},{16,528},{24,536},{32,544},{40,552},{48,560},{56,5... | collective-permute-start | bytes 786440 | tf_op jit(solution)/shard_map/ppermute | solution.py:19
  (5 other events, 3.5 us)
where the time goes:
time: 273 us; the launch traced here: 272 us
  waiting for transfers between devices  104 us (38%)
  starting transfers between devices  87.1 us (32%)
  blocking collectives  38.4 us (14%)
  matrix products  15.7 us (6%)
  local copies, waits for them, and re-layouts  12.7 us (5%)
  other arithmetic  11.6 us (4%)
  between operations  3.06 us (1%)
    ppermute x21, waiting for transfers between devices, partner(): lax.ppermute(x, axis, [(i, i ^ 1 << stride) for i in range(lax.axis_size(...  104 us
    ppermute x21, starting transfers between devices, partner(): lax.ppermute(x, axis, [(i, i ^ 1 << stride) for i in range(lax.axis_size(...  85.1 us
    all_gather x1, blocking collectives, per_device(): lax.all_gather(hidden, 'tp', axis=1, tiled=True)  38.4 us
    unnamed x31, local copies, waits for them, and re-layouts  12.3 us
    dot_general x12, matrix products, apply_table(): jnp.einsum('km,emw->ekw', table, values, precision=lax.Precision.HIGHEST)  9.51 us
    another operation x20, other arithmetic  7.73 us
  transfers between devices with their start and end apart: 22, of which 14 were waited for; matrix products, arithmetic and copies ran while one was open for 3% of the time, Pallas kernels for 0%

commit v1 on v0

v1 whole, which is shorter than its diff:
```python
import functools

import jax
import jax.numpy as jnp
from jax import lax
from jax.experimental import pallas as pl
from jax.experimental.pallas import tpu as pltpu
from jax.sharding import PartitionSpec as P

MESH = pl.DeviceIdType.MESH
NX = 16
NY = 8
NZ = 8
ROWS = 128
CHAN = 256
MODEL = 4096
FEATS = 512
KCH = 1024
NK = MODEL // KCH
TOEP = 16512


def kernel(
    x_hbm, w_hbm, taps_hbm, filt_hbm, skip_hbm, o_hbm, out_ref,
    xb, wb, ob, taps_v, filt_v, skip_v,
    pacc, halo_s, halo_r, ext, gated_v, query_v,
    fs, fr, hs, hr, toep, perm1, perm2, sel, lhs,
    xs, xr, ys, yr, acc, ys2, yr2, xs2, xr2, hid, oacc,
    in_sem, w_sem, halo_sem, f_sem, h_sem, x_sem, y_sem, y2_sem, x2_sem, zr_sem, zl_sem,
):
    f32, bf16 = jnp.float32, jnp.bfloat16
    ctx = lax.axis_index("ctx")
    z = lax.axis_index("tp")
    y, xc = ctx // NX, ctx % NX
    nxt, prv = (ctx + 1) % (NX * NY), (ctx + NX * NY - 1) % (NX * NY)
    zp, zm = (z + 1) % NZ, (z + NZ - 1) % NZ

    def rowpeer(o):
        return (xc + o) % NX

    def colpeer(o):
        return (y + o) % NY

    copies = [
        pltpu.make_async_copy(x_hbm, xb, in_sem.at[0]),
        pltpu.make_async_copy(taps_hbm, taps_v, in_sem.at[1]),
        pltpu.make_async_copy(filt_hbm, filt_v, in_sem.at[2]),
        pltpu.make_async_copy(skip_hbm, skip_v, in_sem.at[3]),
        pltpu.make_async_copy(o_hbm, ob, in_sem.at[4]),
    ]

    def wcopy(j, c):
        at = pl.ds(c * KCH, KCH)
        return pltpu.make_async_copy(w_hbm.at[j, at], wb.at[j, at], w_sem.at[j, c])

    copies[2].start()
    copies[0].start()
    for j in (1, 2, 0):
        for c in range(NK):
            wcopy(j, c).start()
    copies[1].start()
    copies[3].start()
    copies[4].start()

    barrier = pltpu.get_barrier_semaphore()
    for o in range(1, NX):
        pl.semaphore_signal(barrier, inc=1, device_id=(y * NX + rowpeer(o), z), device_id_type=MESH)
    for o in range(1, NY):
        pl.semaphore_signal(barrier, inc=1, device_id=(colpeer(o) * NX + xc, z), device_id_type=MESH)
    for peer in ((ctx, zp), (ctx, zm), (nxt, z), (prv, z)):
        pl.semaphore_signal(barrier, inc=1, device_id=peer, device_id_type=MESH)

    copies[2].wait()
    for f in range(NX):
        fs[f] = filt_v[f : f + 1, :]

    pl.semaphore_wait(barrier, NX - 1 + NY - 1 + 4)

    def send(src, dst, sems, k_send, k_recv, c, t):
        return pltpu.make_async_remote_copy(
            src_ref=src, dst_ref=dst, send_sem=sems.at[0, k_send], recv_sem=sems.at[1, k_recv],
            device_id=(c, t), device_id_type=MESH)

    sent = []

    def go(copy):
        copy.start()
        sent.append(copy)

    order_x = (8, 7, 9, 6, 10, 5, 11, 4, 12, 3, 13, 2, 14, 1, 15)
    order_y = (4, 3, 5, 2, 6, 1, 7)

    def row_exchange(src, dst, sems):
        for o in order_x:
            p = rowpeer(o)
            go(send(src.at[p], dst.at[xc], sems, o, o, y * NX + p, z))

    def row_arrive(dst, sems):
        for o in order_x:
            p = (xc + NX - o) % NX
            send(dst.at[p], dst.at[p], sems, o, o, ctx, z).wait_recv()

    def col_exchange(src_of, dst, sems):
        for o in order_y:
            p = colpeer(o)
            go(send(src_of(p), dst.at[y], sems, o, o, p * NX + xc, z))

    def col_arrive(dst, sems):
        for o in order_y:
            p = (y + NY - o) % NY
            send(dst.at[p], dst.at[p], sems, o, o, ctx, z).wait_recv()

    row_exchange(fs, fr, f_sem)
    fr[xc] = fs[xc]

    copies[0].wait()
    pacc[...] = jnp.zeros_like(pacc)

    def project(j):
        @pl.loop(0, NK)
        def _(c):
            wcopy(j, c).wait()
            at = pl.ds(pl.multiple_of(c * KCH, KCH), KCH)
            pacc[j] += jnp.dot(xb[:, at], wb[j, at, :], preferred_element_type=f32)

        rounded = pacc[j].astype(bf16)
        ext[j, 8:, :] = rounded.astype(f32)
        halo_s[j] = rounded[ROWS - 8 :, :]

    def halo(j):
        return send(halo_s.at[j], halo_r.at[j], halo_sem, j, j, nxt, z)

    def short_conv(j):
        send(halo_r.at[j], halo_r.at[j], halo_sem, j, j, ctx, z).wait_recv()
        before = halo_r[j].astype(f32)
        ext[j, :8, :] = jnp.where(ctx == 0, jnp.zeros_like(before), before)
        taps = [taps_v[i].astype(f32)[j : j + 1, :] for i in range(3)]
        return (
            taps[0] * ext[j, 8:, :]
            + taps[1] * ext[j, 7 : 7 + ROWS, :]
            + taps[2] * ext[j, 6 : 6 + ROWS, :]
        )

    project(1)
    go(halo(1))
    project(2)
    go(halo(2))
    copies[1].wait()
    keyed = short_conv(1)
    gated = keyed * short_conv(2)
    gated_v[...] = gated
    xs[...] = gated.T.astype(bf16).reshape(NX, 16, ROWS)
    row_exchange(xs, xr, x_sem)
    xr[xc] = xs[xc]

    row_arrive(fr, f_sem)
    hs[...] = fr[...].reshape(NX, ROWS)
    col_exchange(lambda p: hs, hr, h_sem)
    hr[y] = hs[...]

    row = lax.broadcasted_iota(jnp.int32, (256, 256), 0)
    col = lax.broadcasted_iota(jnp.int32, (256, 256), 1)
    perm1[...] = jnp.where(col == (row // 2 % 16) * 16 + row // 32 * 2 + row % 2, 1.0, 0.0).astype(bf16)
    row = lax.broadcasted_iota(jnp.int32, (128, 128), 0)
    col = lax.broadcasted_iota(jnp.int32, (128, 128), 1)
    perm2[...] = jnp.where(col == (row % 16 // 2) * 16 + row // 16 * 2 + row % 2, 1.0, 0.0).astype(bf16)
    row = lax.broadcasted_iota(jnp.int32, (128, 256), 0)
    col = lax.broadcasted_iota(jnp.int32, (128, 256), 1)
    base = row // 2 * 4 + row % 2 - col

    @pl.loop(0, 16)
    def _(b):
        shift = (7 - b // 2) * 4 - b % 2 * 2
        sel[pl.ds(pl.multiple_of(b * 128, 128), 128), :] = jnp.where(base == shift, 1.0, 0.0).astype(bf16)

    project(0)
    go(halo(0))
    query_v[...] = short_conv(0)

    row_arrive(xr, x_sem)
    ys[...] = jnp.dot(
        perm1[...], xr[...].reshape(256, ROWS), preferred_element_type=f32
    ).astype(bf16).reshape(NY, 32, ROWS)
    col_exchange(lambda p: ys.at[p], yr, y_sem)
    yr[y] = ys[y]

    col_arrive(hr, h_sem)
    lane = lax.broadcasted_iota(jnp.int32, (128, 128), 1)
    sub = lax.broadcasted_iota(jnp.int32, (128, 128), 0)
    keep = lane >= sub
    toep[128 * 128 :, :] = jnp.zeros((128, 128), bf16)

    def toeplitz(q, before):
        line = hr[q // 16, pl.ds(q % 16, 1), :]
        now = pltpu.roll(jnp.broadcast_to(line, (128, 128)), 0, 1, stride=1, stride_axis=0)
        at = pl.multiple_of((127 - q) * 128, 128)
        toep[pl.ds(at, 128), :] = jnp.where(keep, now, before).astype(bf16)
        return now

    lax.fori_loop(0, 128, toeplitz, jnp.zeros((128, 128), f32))

    col_arrive(yr, y_sem)
    lhs[:128, :] = jnp.zeros((128, 2048), bf16)
    seq = yr[...].reshape(256, ROWS)
    for b in range(16):
        lhs[128:, b * 128 : (b + 1) * 128] = jnp.dot(
            sel[b * 128 : (b + 1) * 128, :], seq, preferred_element_type=f32
        ).astype(bf16)
    acc[...] = jnp.zeros_like(acc)

    @pl.loop(0, 8)
    def _(k):
        r0 = pl.multiple_of(14464 - k * 2048, 128)
        r1 = pl.multiple_of(14336 - k * 2048, 128)
        left = lhs[pl.ds(pl.multiple_of(128 - k * 16, 16), 128), :]
        right = jnp.concatenate([toep[pl.ds(r0, 2048), :], toep[pl.ds(r1, 2048), :]], axis=1)
        acc[...] += jnp.dot(left, right, preferred_element_type=f32)

    ys2[...] = acc[...].astype(bf16).reshape(NY, 16, 256)
    col_exchange(lambda p: ys2.at[p], yr2, y2_sem)
    yr2[y] = ys2[y]
    col_arrive(yr2, y2_sem)
    back = jnp.dot(
        perm2[...], yr2[...].reshape(128, 256), preferred_element_type=f32
    ).astype(bf16)
    for b in range(8):
        for par in range(2):
            xs2[2 * b + par] = back[16 * b : 16 * b + 16, 128 * par : 128 * par + 128]
    row_exchange(xs2, xr2, x2_sem)
    xr2[xc] = xs2[xc]
    copies[3].wait()
    row_arrive(xr2, x2_sem)
    conv = xr2[...].reshape(CHAN, ROWS).astype(f32).T
    hid[z] = (query_v[...] * (conv + skip_v[...] * gated_v[...])).astype(bf16)

    copies[4].wait()
    half = ROWS // 2

    def zcopy(step, part, sems, to):
        b = (z + NZ - step) % NZ if sems is zr_sem else (z + step) % NZ
        at = hid.at[b, pl.ds(part * half, half)]
        return send(at, at, sems, step * 2 + part, step * 2 + part, ctx, to)

    def arrived(step, part, sems):
        b = (z + NZ - step - 1) % NZ if sems is zr_sem else (z + step + 1) % NZ
        at = hid.at[b, pl.ds(part * half, half)]
        send(at, at, sems, step * 2 + part, step * 2 + part, ctx, z).wait_recv()

    def out_part(b):
        at = pl.ds(pl.multiple_of(b * CHAN, CHAN), CHAN)
        return jnp.dot(hid[b], ob[at, :], preferred_element_type=f32)

    for part in range(2):
        go(zcopy(0, part, zr_sem, zp))
        go(zcopy(0, part, zl_sem, zm))
    oacc[...] = out_part(z)
    for step in range(3):
        for part in range(2):
            arrived(step, part, zr_sem)
            if step < 2 or part == 0:
                go(zcopy(step + 1, part, zr_sem, zp))
            arrived(step, part, zl_sem)
            if step < 2 or part == 1:
                go(zcopy(step + 1, part, zl_sem, zm))
        oacc[...] += out_part((z + NZ - step - 1) % NZ)
        oacc[...] += out_part((z + step + 1) % NZ)
    arrived(3, 0, zr_sem)
    arrived(3, 1, zl_sem)
    out_ref[...] = (oacc[...] + out_part((z + 4) % NZ)).astype(bf16)
    for copy in sent:
        copy.wait_send()


def per_device(hidden_in, in_proj, short_taps, long_filters, skip_gain, out_proj):
    f32, bf16 = jnp.float32, jnp.bfloat16
    VMEM, DMA = pltpu.VMEM, pltpu.SemaphoreType.DMA
    scratch = [
        VMEM((ROWS, MODEL), bf16),
        VMEM((3, MODEL, CHAN), bf16),
        VMEM((NZ * CHAN, FEATS), bf16),
        VMEM((3, 3, CHAN), bf16),
        VMEM((NX, ROWS), f32),
        VMEM((1, CHAN), f32),
        VMEM((3, ROWS, CHAN), f32),
        VMEM((3, 8, CHAN), bf16),
        VMEM((3, 8, CHAN), bf16),
        VMEM((3, ROWS + 8, CHAN), f32),
        VMEM((ROWS, CHAN), f32),
        VMEM((ROWS, CHAN), f32),
        VMEM((NX, 1, ROWS), f32),
        VMEM((NX, 1, ROWS), f32),
        VMEM((NX, ROWS), f32),
        VMEM((NY, NX, ROWS), f32),
        VMEM((TOEP, 128), bf16),
        VMEM((256, 256), bf16),
        VMEM((128, 128), bf16),
        VMEM((2048, 256), bf16),
        VMEM((256, 2048), bf16),
        VMEM((NX, 16, ROWS), bf16),
        VMEM((NX, 16, ROWS), bf16),
        VMEM((NY, 32, ROWS), bf16),
        VMEM((NY, 32, ROWS), bf16),
        VMEM((128, 256), f32),
        VMEM((NY, 16, 256), bf16),
        VMEM((NY, 16, 256), bf16),
        VMEM((NX, 16, ROWS), bf16),
        VMEM((NX, 16, ROWS), bf16),
        VMEM((NZ, ROWS, CHAN), bf16),
        VMEM((ROWS, FEATS), f32),
        DMA((5,)),
        DMA((3, NK)),
        DMA((2, 3)),
        DMA((2, NX)),
        DMA((2, NY)),
        DMA((2, NX)),
        DMA((2, NY)),
        DMA((2, NY)),
        DMA((2, NX)),
        DMA((2, 8)),
        DMA((2, 8)),
    ]
    return pl.pallas_call(
        kernel,
        out_shape=jax.ShapeDtypeStruct((ROWS, FEATS), bf16),
        in_specs=[pl.BlockSpec(memory_space=pl.ANY)] * 6,
        out_specs=pl.BlockSpec(memory_space=pltpu.VMEM),
        scratch_shapes=scratch,
        compiler_params=pltpu.CompilerParams(
            collective_id=0, has_side_effects=True, vmem_limit_bytes=48 * 1024 * 1024
        ),
    )(
        hidden_in,
        jnp.transpose(in_proj, (1, 0, 2)),
        short_taps,
        long_filters.T,
        skip_gain.reshape(1, CHAN),
        out_proj,
    )


def solution(mesh):
    in_specs = (
        P("ctx", None),
        P(None, None, "tp"),
        P(None, None, "tp"),
        P("ctx", "tp"),
        P("tp"),
        P(None, "tp"),
    )
    return jax.shard_map(
        per_device, mesh=mesh, in_specs=in_specs, out_specs=P("ctx", "tp"), check_vma=False
    )
```

time: 273 us -> 76 us (0.28)
  the two profiles are of different devices: /device:TPU:14 before, /device:TPU:2 now
where the time goes in v1:
time: 76 us; the launch traced here: 75.7 us
  Pallas kernels  70.2 us (92%)
  local copies, waits for them, and re-layouts  5.54 us (7%)
    pallas_call x1, Pallas kernels, per_device(): pl.pallas_call(kernel, out_shape=jax.ShapeDtypeStruct((ROWS, FEATS), bf16...  70.2 us
    unnamed x11, local copies, waits for them, and re-layouts  5.54 us

profile of v1, /device:TPU:2, one launch (start us, length us, event | category | flops | bytes accessed | tf_op | source)
XLA Modules:
  0.0 75.7 jit_solution(4694269975493848552)
XLA Ops:
  0.0 0.0 copy-start
  0.0 1.6 %copy-done = bf16[2048,512]{1,0:T(8,128)(2,1)S(1)} copy-done((bf16[2048,512]{1,0:T(8,128)(2,1)S(1)}, bf16[2048,512]{1,0:T(8,128)(2,1)}, u32[]{:S(2)}) %copy-start) | copy-done | bytes 2097176
  1.6 0.0 copy-start.1
  1.6 1.2 %copy-done.1 = bf16[128,4096]{1,0:T(8,128)(2,1)S(1)} copy-done((bf16[128,4096]{1,0:T(8,128)(2,1)S(1)}, bf16[128,4096]{1,0:T(8,128)(2,1)}, u32[]{:S(2)}) %copy-start.1) | copy-done | bytes 1048600
  2.8 0.0 copy-start.2
  2.8 0.7 copy-done.2
  3.5 0.0 copy-start.3
  3.5 0.7 copy-done.3
  4.2 0.0 copy-start.4
  4.2 0.7 copy-done.4
  4.9 70.2 %shard_map.64 = bf16[128,512]{1,0:T(8,128)(2,1)S(1)} custom-call(bf16[128,4096]{1,0:T(8,128)(2,1)S(1)} %copy-done.1, bf16[3,4096,256]{2,1,0:T(8,128)(2,1)} %bitcast.5, bf16[3,3,256]{2,1,0:T(4,128)(2,1)S(1)} %copy-done.3, f32[16,128]{1,0:T(8,128)S(1)} %bitcast.3, f32[1,256]{1,0:T(1,128)S(1)} %bitcast.4, bf16[2048,512]{1,0:T(8,128)(2,1)S(1)} %copy-done), custom_call_target="tpu_custom_call" | custom-call | tf_op jit(solution)/shard_map/pallas_call | solution.py:322
  75.1 0.7 copy.8
Async XLA Ops:
  0.0 1.6 %copy-start = (bf16[2048,512]{1,0:T(8,128)(2,1)S(1)}, bf16[2048,512]{1,0:T(8,128)(2,1)}, u32[]{:S(2)}) copy-start(bf16[2048,512]{1,0:T(8,128)(2,1)} %o_hbm.1) | copy-start | bytes 6291460
  1.6 1.2 %copy-start.1 = (bf16[128,4096]{1,0:T(8,128)(2,1)S(1)}, bf16[128,4096]{1,0:T(8,128)(2,1)}, u32[]{:S(2)}) copy-start(bf16[128,4096]{1,0:T(8,128)(2,1)} %x_hbm.1) | copy-start | bytes 3145732
  2.8 0.7 copy-start.2
  3.5 0.7 copy-start.3
  4.2 0.7 copy-start.4

commit v2 on v1

v2 whole, which is shorter than its diff:
```python
import functools

import jax
import jax.numpy as jnp
from jax import lax
from jax.experimental import pallas as pl
from jax.experimental.pallas import tpu as pltpu
from jax.sharding import PartitionSpec as P

MESH = pl.DeviceIdType.MESH
NX = 16
NY = 8
NZ = 8
ROWS = 128
CHAN = 256
MODEL = 4096
FEATS = 512
KCH = 1024
NK = MODEL // KCH
TOEP = 16512


def kernel(
    x_hbm, w_hbm, taps_hbm, filt_hbm, skip_hbm, o_hbm, out_ref,
    xb, wb, ob, taps_v, filt_v, skip_v,
    pacc, halo_s, halo_r, ext, query_t, direct_t,
    fs, fr, hs, hr, toep, perm1, perm2, lhs,
    xs, xr, ys, yr, acc, ys2, yr2, xs2, xr2, hid, oacc,
    in_sem, w_sem, o_sem, halo_sem, f_sem, h_sem, x_sem, y_sem, y2_sem, x2_sem, zr_sem, zl_sem,
):
    f32, bf16 = jnp.float32, jnp.bfloat16
    ctx = lax.axis_index("ctx")
    z = lax.axis_index("tp")
    y, xc = ctx // NX, ctx % NX
    x, core = xc // 2, xc % 2
    nxt, prv = (ctx + 1) % (NX * NY), (ctx + NX * NY - 1) % (NX * NY)
    zp, zm = (z + 1) % NZ, (z + NZ - 1) % NZ

    away = (0, 1, -1, 2, -2, 3, -3, 4)
    slot_of = {(dx, dc): 2 * k + dc for k, dx in enumerate(away) for dc in range(2)}
    back_of = {(dx, dc): slot_of[(4 if dx == 4 else -dx, dc)] for dx, dc in slot_of}
    row_peers = [key for key in slot_of if key != (0, 0)]
    far_first = row_peers[::-1]

    def rowpeer(key):
        return (x + key[0] + 8) % 8 * 2 + (core + key[1]) % 2

    def colpeer(o):
        return (y + o) % NY

    copies = [
        pltpu.make_async_copy(x_hbm, xb, in_sem.at[0]),
        pltpu.make_async_copy(taps_hbm, taps_v, in_sem.at[1]),
        pltpu.make_async_copy(filt_hbm, filt_v, in_sem.at[2]),
        pltpu.make_async_copy(skip_hbm, skip_v, in_sem.at[3]),
    ]

    def wcopy(j, c):
        at = pl.ds(c * KCH, KCH)
        return pltpu.make_async_copy(w_hbm.at[j, at], wb.at[j, at], w_sem.at[j, c])

    def ocopy(key):
        k = slot_of[key]
        return pltpu.make_async_copy(o_hbm.at[:, rowpeer(key)], ob.at[:, k], o_sem.at[k])

    copies[0].start()
    for j in (1, 2):
        for c in range(NK):
            wcopy(j, c).start()
    copies[2].start()
    copies[1].start()
    copies[3].start()

    barrier = pltpu.get_barrier_semaphore()
    for key in far_first:
        pl.semaphore_signal(barrier, inc=1, device_id=(y * NX + rowpeer(key), z), device_id_type=MESH)
    for o in (4, 3, 5, 2, 6, 1, 7):
        pl.semaphore_signal(barrier, inc=1, device_id=(colpeer(o) * NX + xc, z), device_id_type=MESH)
    for peer in ((ctx, zp), (ctx, zm), (nxt, z), (prv, z)):
        pl.semaphore_signal(barrier, inc=1, device_id=peer, device_id_type=MESH)

    row = lax.broadcasted_iota(jnp.int32, (256, 256), 0)
    col = lax.broadcasted_iota(jnp.int32, (256, 256), 1)
    take = (row % 16 // 2 * 2 + row // 16 % 2) * 16 + row // 32 * 2 + row % 2
    perm1[...] = jnp.where(col == take, 1.0, 0.0).astype(bf16)
    row = lax.broadcasted_iota(jnp.int32, (128, 128), 0)
    col = lax.broadcasted_iota(jnp.int32, (128, 128), 1)
    perm2[...] = jnp.where(col == (row % 16 // 2) * 16 + row // 16 * 2 + row % 2, 1.0, 0.0).astype(bf16)
    pacc[...] = jnp.zeros_like(pacc)
    acc[...] = jnp.zeros_like(acc)
    for k in range(1, 8):
        lhs[: 16 * k, k * 256 : (k + 1) * 256] = jnp.zeros((16 * k, 256), bf16)
    toep[128 * 128 :, :] = jnp.zeros((128, 128), bf16)

    def send(src, dst, sems, k_send, k_recv, c, t):
        return pltpu.make_async_remote_copy(
            src_ref=src, dst_ref=dst, send_sem=sems.at[0, k_send], recv_sem=sems.at[1, k_recv],
            device_id=(c, t), device_id_type=MESH)

    sent = []

    def go(copy):
        copy.start()
        sent.append(copy)

    def row_exchange(src, dst_of, sems):
        for key in far_first:
            p = rowpeer(key)
            go(send(src.at[p], dst_of(key), sems, slot_of[key], back_of[key], y * NX + p, z))

    def row_arrive(dst, sems):
        for key in row_peers:
            at = dst.at[rowpeer(key)]
            send(at, at, sems, slot_of[key], slot_of[key], ctx, z).wait_recv()

    def col_exchange(src_of, dst, sems):
        for o in (4, 3, 5, 2, 6, 1, 7):
            p = colpeer(o)
            go(send(src_of(p), dst.at[y], sems, o, o, p * NX + xc, z))

    def col_wait(p, dst, sems):
        o = (y + NY - p) % NY
        send(dst.at[p], dst.at[p], sems, o, o, ctx, z).wait_recv()

    def col_arrive(dst, sems):
        for o in (7, 1, 6, 2, 5, 3, 4):
            col_wait((y + NY - o) % NY, dst, sems)

    copies[0].wait()

    def project(j):
        @pl.loop(0, NK)
        def _(c):
            wcopy(j, c).wait()
            at = pl.ds(pl.multiple_of(c * KCH, KCH), KCH)
            pacc[j] += jnp.dot(xb[:, at], wb[j, at, :], preferred_element_type=f32)

        rounded = pacc[j].astype(bf16)
        ext[j, 8:, :] = rounded.astype(f32)
        halo_s[j] = rounded[ROWS - 8 :, :]

    def halo(j):
        return send(halo_s.at[j], halo_r.at[j], halo_sem, j, j, nxt, z)

    def short_conv(j):
        send(halo_r.at[j], halo_r.at[j], halo_sem, j, j, ctx, z).wait_recv()
        before = halo_r[j].astype(f32)
        ext[j, :8, :] = jnp.where(ctx == 0, jnp.zeros_like(before), before)
        taps = [taps_v[i].astype(f32)[j : j + 1, :] for i in range(3)]
        return (
            taps[0] * ext[j, 8:, :]
            + taps[1] * ext[j, 7 : 7 + ROWS, :]
            + taps[2] * ext[j, 6 : 6 + ROWS, :]
        )

    project(1)
    project(2)
    for c in range(NK):
        wcopy(0, c).start()
    pl.semaphore_wait(barrier, NX - 1 + NY - 1 + 4)
    go(halo(1))
    go(halo(2))

    copies[2].wait()
    for f in range(NX):
        fs[f] = filt_v[f : f + 1, :]
    row_exchange(fs, lambda key: fr.at[xc], f_sem)
    fr[xc] = fs[xc]
    copies[1].wait()
    copies[3].wait()
    keyed = short_conv(1)
    gated = keyed * short_conv(2)
    xs[...] = gated.T.astype(bf16).reshape(NX, 16, ROWS)
    row_exchange(xs, lambda key: xr.at[xc], x_sem)
    xr[xc] = xs[xc]
    direct_t[...] = (skip_v[...] * gated).T
    for key in slot_of:
        ocopy(key).start()

    project(0)
    go(halo(0))

    row_arrive(fr, f_sem)
    hs[...] = fr[...].reshape(NX, ROWS)
    col_exchange(lambda p: hs, hr, h_sem)
    hr[y] = hs[...]

    row_arrive(xr, x_sem)
    ys[...] = jnp.dot(
        perm1[...], xr[...].reshape(256, ROWS), preferred_element_type=f32
    ).astype(bf16).reshape(NY, 2, 16, ROWS)
    col_exchange(lambda p: ys.at[p], yr, y_sem)
    yr[y] = ys[y]

    lane = lax.broadcasted_iota(jnp.int32, (128, 128), 1)
    sub = lax.broadcasted_iota(jnp.int32, (128, 128), 0)
    keep = lane >= sub

    def toeplitz(p, before):
        @pl.when(p != y)
        def _():
            col_wait(p, hr, h_sem)

        for j in range(16):
            line = hr[p, j : j + 1, :]
            now = pltpu.roll(jnp.broadcast_to(line, (128, 128)), 0, 1, stride=1, stride_axis=0)
            at = pl.multiple_of((127 - j) * 128 - p * 2048, 128)
            toep[pl.ds(at, 128), :] = jnp.where(keep, now, before).astype(bf16)
            before = now
        return before

    lax.fori_loop(0, NY, toeplitz, jnp.zeros((128, 128), f32))

    col_arrive(yr, y_sem)
    for k in range(8):
        for p in range(8 - k):
            for par in range(2):
                at = k * 256 + par * 128
                lhs[16 * (p + k) : 16 * (p + k + 1), at : at + 128] = yr[p, par]

    @pl.loop(0, 8)
    def _(i):
        right = []
        for k in range(8):
            r0 = pl.multiple_of(14464 - 2048 * k + 256 * i, 128)
            r1 = pl.multiple_of(14336 - 2048 * k + 256 * i, 128)
            right.append(jnp.concatenate([toep[pl.ds(r0, 256), :], toep[pl.ds(r1, 256), :]], axis=1))
        acc[8:, :] = acc[6 : 6 + 128, :] + jnp.dot(
            lhs[...], jnp.concatenate(right, axis=0), preferred_element_type=f32
        )

    ys2[...] = acc[8:, :].astype(bf16).reshape(NY, 16, 256)
    col_exchange(lambda p: ys2.at[p], yr2, y2_sem)
    yr2[y] = ys2[y]
    query_t[...] = short_conv(0).T
    for key in slot_of:
        ocopy(key).wait()
    col_arrive(yr2, y2_sem)
    back = jnp.dot(
        perm2[...], yr2[...].reshape(128, 256), preferred_element_type=f32
    ).astype(bf16)
    for b in range(8):
        for par in range(2):
            xs2[2 * b + par] = back[16 * b : 16 * b + 16, 128 * par : 128 * par + 128]
    row_exchange(xs2, lambda key: xr2.at[back_of[key]], x2_sem)
    xr2[0] = xs2[xc]

    def own(g):
        for k in range(4 * g, 4 * g + 4):
            key = (away[k // 2], k % 2)
            if key != (0, 0):
                send(xr2.at[k], xr2.at[k], x2_sem, k, k, ctx, z).wait_recv()
            at = pl.ds(pl.multiple_of(rowpeer(key) * 16, 16), 16)
            hid[z, k] = (query_t[at, :] * (xr2[k].astype(f32) + direct_t[at, :])).astype(bf16)
        forward(0, g)

    def part(b, g):
        return hid.at[b, pl.ds(4 * g, 4)]

    def forward(d, g):
        if d < 3 or g % 2 == 0:
            at = part((z + NZ - d) % NZ, g)
            go(send(at, at, zr_sem, 4 * d + g, 4 * d + g, ctx, zp))
        if d < 3 or g % 2 == 1:
            at = part((z + d) % NZ, g)
            go(send(at, at, zl_sem, 4 * d + g, 4 * d + g, ctx, zm))

    def arrive(d, g):
        k = 4 * (d - 1) + g
        if d < 4 or g % 2 == 0:
            at = part((z + NZ - d) % NZ, g)
            send(at, at, zr_sem, k, k, ctx, z).wait_recv()
        if d < 4 or g % 2 == 1:
            at = part((z + d) % NZ, g)
            send(at, at, zl_sem, k, k, ctx, z).wait_recv()
        if d < 4:
            forward(d, g)

    def out_part(b):
        return lax.dot_general(
            hid[b].reshape(CHAN, ROWS), ob[b].reshape(CHAN, FEATS),
            (((0,), (0,)), ((), ())), preferred_element_type=f32)

    ready, hop = (1.2, 2.5, 3.7, 5.0), 1.9
    events = sorted((ready[g] + hop * d, d, g) for d in range(5) for g in range(4))
    for _, d, g in events:
        if d == 0:
            own(g)
        else:
            arrive(d, g)
        if g == 3:
            if d == 0:
                oacc[...] = out_part(z)
            elif d < 4:
                oacc[...] += out_part((z + NZ - d) % NZ) + out_part((z + d) % NZ)
    out_ref[...] = (oacc[...] + out_part((z + 4) % NZ)).astype(bf16)
    for copy in sent:
        copy.wait_send()


def per_device(hidden_in, in_proj, short_taps, long_filters, skip_gain, out_proj):
    f32, bf16 = jnp.float32, jnp.bfloat16
    VMEM, DMA = pltpu.VMEM, pltpu.SemaphoreType.DMA
    scratch = [
        VMEM((ROWS, MODEL), bf16),
        VMEM((3, MODEL, CHAN), bf16),
        VMEM((NZ, NX, 16, FEATS), bf16),
        VMEM((3, 3, CHAN), bf16),
        VMEM((NX, ROWS), f32),
        VMEM((1, CHAN), f32),
        VMEM((3, ROWS, CHAN), f32),
        VMEM((3, 8, CHAN), bf16),
        VMEM((3, 8, CHAN), bf16),
        VMEM((3, ROWS + 8, CHAN), f32),
        VMEM((CHAN, ROWS), f32),
        VMEM((CHAN, ROWS), f32),
        VMEM((NX, 1, ROWS), f32),
        VMEM((NX, 1, ROWS), f32),
        VMEM((NX, ROWS), f32),
        VMEM((NY, NX, ROWS), f32),
        VMEM((TOEP, 128), bf16),
        VMEM((256, 256), bf16),
        VMEM((128, 128), bf16),
        VMEM((128, 2048), bf16),
        VMEM((NX, 16, ROWS), bf16),
        VMEM((NX, 16, ROWS), bf16),
        VMEM((NY, 2, 16, ROWS), bf16),
        VMEM((NY, 2, 16, ROWS), bf16),
        VMEM((136, 256), f32),
        VMEM((NY, 16, 256), bf16),
        VMEM((NY, 16, 256), bf16),
        VMEM((NX, 16, ROWS), bf16),
        VMEM((NX, 16, ROWS), bf16),
        VMEM((NZ, NX, 16, ROWS), bf16),
        VMEM((ROWS, FEATS), f32),
        DMA((4,)),
        DMA((3, NK)),
        DMA((NX,)),
        DMA((2, 3)),
        DMA((2, NX)),
        DMA((2, NY)),
        DMA((2, NX)),
        DMA((2, NY)),
        DMA((2, NY)),
        DMA((2, NX)),
        DMA((2, 16)),
        DMA((2, 16)),
    ]
    return pl.pallas_call(
        kernel,
        out_shape=jax.ShapeDtypeStruct((ROWS, FEATS), bf16),
        in_specs=[pl.BlockSpec(memory_space=pl.ANY)] * 6,
        out_specs=pl.BlockSpec(memory_space=pltpu.VMEM),
        scratch_shapes=scratch,
        compiler_params=pltpu.CompilerParams(
            collective_id=0, has_side_effects=True, vmem_limit_bytes=67043328
        ),
    )(
        hidden_in,
        jnp.transpose(in_proj, (1, 0, 2)),
        short_taps,
        long_filters.T,
        skip_gain.reshape(1, CHAN),
        out_proj.reshape(NZ, NX, 16, FEATS),
    )


def solution(mesh):
    in_specs = (
        P("ctx", None),
        P(None, None, "tp"),
        P(None, None, "tp"),
        P("ctx", "tp"),
        P("tp"),
        P(None, "tp"),
    )
    return jax.shard_map(
        per_device, mesh=mesh, in_specs=in_specs, out_specs=P("ctx", "tp"), check_vma=False
    )
```

time: 76 us -> 67.9 us (0.89)
  the two profiles are of different devices: /device:TPU:2 before, /device:TPU:6 now
where the time goes in v2:
time: 67.9 us; the launch traced here: 67.7 us
  Pallas kernels  66.1 us (97%)
  local copies, waits for them, and re-layouts  1.57 us (2%)
    pallas_call x1, Pallas kernels, per_device(): pl.pallas_call(kernel, out_shape=jax.ShapeDtypeStruct((ROWS, FEATS), bf16...  66.1 us
    unnamed x1, local copies, waits for them, and re-layouts  1.57 us

profile of v2, /device:TPU:6, one launch (start us, length us, event | category | flops | bytes accessed | tf_op | source)
XLA Modules:
  0.0 67.7 jit_solution(17684482173449444122)
XLA Ops:
  0.0 66.1 %shard_map.64 = bf16[128,512]{1,0:T(8,128)(2,1)} custom-call(bf16[128,4096]{1,0:T(8,128)(2,1)} %x_hbm.1, bf16[3,4096,256]{2,1,0:T(8,128)(2,1)} %bitcast.4, bf16[3,3,256]{2,1,0:T(4,128)(2,1)} %taps_hbm.1, f32[16,128]{1,0:T(8,128)} %bitcast.6, f32[1,256]{1,0:T(1,128)} %bitcast.7, bf16[8,16,16,512]{3,2,1,0:T(8,128)(2,1)} %bitcast.5), custom_call_target="tpu_custom_call" | custom-call | tf_op jit(solution)/shard_map/pallas_call | solution.py:349
  66.2 1.6 %copy.8 = bf16[128,512]{1,0:T(8,128)(2,1)} copy(bf16[128,512]{1,0:T(8,128)(2,1)} %shard_map.64) | data formatting | bytes 262144

commit v3 on v2

--- a/solution.py
+++ b/solution.py
@@ -26,7 +26,7 @@
     pacc, halo_s, halo_r, ext, query_t, direct_t,
     fs, fr, hs, hr, toep, perm1, perm2, lhs,
     xs, xr, ys, yr, acc, ys2, yr2, xs2, xr2, hid, oacc,
-    in_sem, w_sem, o_sem, halo_sem, f_sem, h_sem, x_sem, y_sem, y2_sem, x2_sem, zr_sem, zl_sem,
+    in_sem, w_sem, o_sem, halo_sem, f_sem, h_sem, x_sem, y_sem, y2_sem, x2_sem, z_sem,
 ):
     f32, bf16 = jnp.float32, jnp.bfloat16
     ctx = lax.axis_index("ctx")
@@ -34,7 +34,7 @@
     y, xc = ctx // NX, ctx % NX
     x, core = xc // 2, xc % 2
     nxt, prv = (ctx + 1) % (NX * NY), (ctx + NX * NY - 1) % (NX * NY)
-    zp, zm = (z + 1) % NZ, (z + NZ - 1) % NZ
+    zm = (z + NZ - 1) % NZ
 
     away = (0, 1, -1, 2, -2, 3, -3, 4)
     slot_of = {(dx, dc): 2 * k + dc for k, dx in enumerate(away) for dc in range(2)}
@@ -61,7 +61,7 @@
 
     def ocopy(key):
         k = slot_of[key]
-        return pltpu.make_async_copy(o_hbm.at[:, rowpeer(key)], ob.at[:, k], o_sem.at[k])
+        return pltpu.make_async_copy(o_hbm.at[:, rowpeer(key)], ob.at[k // 4, :, k % 4], o_sem.at[k])
 
     copies[0].start()
     for j in (1, 2):
@@ -76,8 +76,10 @@
         pl.semaphore_signal(barrier, inc=1, device_id=(y * NX + rowpeer(key), z), device_id_type=MESH)
     for o in (4, 3, 5, 2, 6, 1, 7):
         pl.semaphore_signal(barrier, inc=1, device_id=(colpeer(o) * NX + xc, z), device_id_type=MESH)
-    for peer in ((ctx, zp), (ctx, zm), (nxt, z), (prv, z)):
+    for peer in ((nxt, z), (prv, z)):
         pl.semaphore_signal(barrier, inc=1, device_id=peer, device_id_type=MESH)
+    for o in (4, 3, 5, 2, 6, 1, 7):
+        pl.semaphore_signal(barrier, inc=1, device_id=(ctx, (z + o) % NZ), device_id_type=MESH)
 
     row = lax.broadcasted_iota(jnp.int32, (256, 256), 0)
     col = lax.broadcasted_iota(jnp.int32, (256, 256), 1)
@@ -153,17 +155,17 @@
             + taps[2] * ext[j, 6 : 6 + ROWS, :]
         )
 
+    copies[2].wait()
+    for f in range(NX):
+        fs[f] = filt_v[f : f + 1, :]
     project(1)
     project(2)
     for c in range(NK):
         wcopy(0, c).start()
-    pl.semaphore_wait(barrier, NX - 1 + NY - 1 + 4)
+    pl.semaphore_wait(barrier, NX - 1 + NY - 1 + 2 + NZ - 1)
     go(halo(1))
     go(halo(2))
 
-    copies[2].wait()
-    for f in range(NX):
-        fs[f] = filt_v[f : f + 1, :]
     row_exchange(fs, lambda key: fr.at[xc], f_sem)
     fr[xc] = fs[xc]
     copies[1].wait()
@@ -173,17 +175,15 @@
     xs[...] = gated.T.astype(bf16).reshape(NX, 16, ROWS)
     row_exchange(xs, lambda key: xr.at[xc], x_sem)
     xr[xc] = xs[xc]
-    direct_t[...] = (skip_v[...] * gated).T
-    for key in slot_of:
-        ocopy(key).start()
-
-    project(0)
-    go(halo(0))
 
     row_arrive(fr, f_sem)
     hs[...] = fr[...].reshape(NX, ROWS)
     col_exchange(lambda p: hs, hr, h_sem)
     hr[y] = hs[...]
+
+    project(0)
+    go(halo(0))
+    direct_t[...] = (skip_v[...] * gated).T
 
     row_arrive(xr, x_sem)
     ys[...] = jnp.dot(
@@ -191,6 +191,8 @@
     ).astype(bf16).reshape(NY, 2, 16, ROWS)
     col_exchange(lambda p: ys.at[p], yr, y_sem)
     yr[y] = ys[y]
+    for key in slot_of:
+        ocopy(key).start()
 
     lane = lax.broadcasted_iota(jnp.int32, (128, 128), 1)
     sub = lax.broadcasted_iota(jnp.int32, (128, 128), 0)
@@ -235,6 +237,8 @@
     query_t[...] = short_conv(0).T
     for key in slot_of:
         ocopy(key).wait()
+    while sent:
+        sent.pop(0).wait_send()
     col_arrive(yr2, y2_sem)
     back = jnp.dot(
         perm2[...], yr2[...].reshape(128, 256), preferred_element_type=f32
@@ -245,55 +249,52 @@
     row_exchange(xs2, lambda key: xr2.at[back_of[key]], x2_sem)
     xr2[0] = xs2[xc]
 
+    def block(g, o):
+        return hid.at[g, (z + o) % NZ]
+
+    def zsend(g, o_block, o_to):
+        at = block(g, o_block)
+        k = (o_block - o_to) % NZ
+        return send(at, at, z_sem, g * NZ + o_to, g * NZ + k, ctx, (z + o_to) % NZ)
+
+    def arrive(g, o):
+        at = block(g, o)
+        send(at, at, z_sem, g * NZ + o, g * NZ + o, ctx, z).wait_recv()
+
+    relayed = (0, 1)
+
     def own(g):
         for k in range(4 * g, 4 * g + 4):
             key = (away[k // 2], k % 2)
             if key != (0, 0):
                 send(xr2.at[k], xr2.at[k], x2_sem, k, k, ctx, z).wait_recv()
             at = pl.ds(pl.multiple_of(rowpeer(key) * 16, 16), 16)
-            hid[z, k] = (query_t[at, :] * (xr2[k].astype(f32) + direct_t[at, :])).astype(bf16)
-        forward(0, g)
-
-    def part(b, g):
-        return hid.at[b, pl.ds(4 * g, 4)]
-
-    def forward(d, g):
-        if d < 3 or g % 2 == 0:
-            at = part((z + NZ - d) % NZ, g)
-            go(send(at, at, zr_sem, 4 * d + g, 4 * d + g, ctx, zp))
-        if d < 3 or g % 2 == 1:
-            at = part((z + d) % NZ, g)
-            go(send(at, at, zl_sem, 4 * d + g, 4 * d + g, ctx, zm))
-
-    def arrive(d, g):
-        k = 4 * (d - 1) + g
-        if d < 4 or g % 2 == 0:
-            at = part((z + NZ - d) % NZ, g)
-            send(at, at, zr_sem, k, k, ctx, z).wait_recv()
-        if d < 4 or g % 2 == 1:
-            at = part((z + d) % NZ, g)
-            send(at, at, zl_sem, k, k, ctx, z).wait_recv()
-        if d < 4:
-            forward(d, g)
-
-    def out_part(b):
+            hid[g, z, k - 4 * g] = (query_t[at, :] * (xr2[k].astype(f32) + direct_t[at, :])).astype(bf16)
+        for o in (4, 3, 5, 2, 6, 1, 7):
+            if o != 4 or g not in relayed:
+                go(zsend(g, 0, o))
+
+    def relay(g):
+        arrive(g, 3)
+        at = block(g, 3)
+        go(send(at, at, z_sem, g * NZ + 4, g * NZ + 4, ctx, zm))
+
+    def out_part(g):
+        for o in (1, 7, 2, 6, 3, 5, 4):
+            if o != 3 or g not in relayed:
+                arrive(g, o)
         return lax.dot_general(
-            hid[b].reshape(CHAN, ROWS), ob[b].reshape(CHAN, FEATS),
+            hid[g].reshape(NZ * 64, ROWS), ob[g].reshape(NZ * 64, FEATS),
             (((0,), (0,)), ((), ())), preferred_element_type=f32)
 
-    ready, hop = (1.2, 2.5, 3.7, 5.0), 1.9
-    events = sorted((ready[g] + hop * d, d, g) for d in range(5) for g in range(4))
-    for _, d, g in events:
-        if d == 0:
-            own(g)
-        else:
-            arrive(d, g)
-        if g == 3:
-            if d == 0:
-                oacc[...] = out_part(z)
-            elif d < 4:
-                oacc[...] += out_part((z + NZ - d) % NZ) + out_part((z + d) % NZ)
-    out_ref[...] = (oacc[...] + out_part((z + 4) % NZ)).astype(bf16)
+    for g in range(4):
+        own(g)
+    for g in relayed:
+        relay(g)
+    oacc[...] = out_part(0)
+    oacc[...] += out_part(1)
+    oacc[...] += out_part(2)
+    out_ref[...] = (oacc[...] + out_part(3)).astype(bf16)
     for copy in sent:
         copy.wait_send()
 
@@ -304,7 +305,7 @@
     scratch = [
         VMEM((ROWS, MODEL), bf16),
         VMEM((3, MODEL, CHAN), bf16),
-        VMEM((NZ, NX, 16, FEATS), bf16),
+        VMEM((4, NZ, 4, 16, FEATS), bf16),
         VMEM((3, 3, CHAN), bf16),
         VMEM((NX, ROWS), f32),
         VMEM((1, CHAN), f32),
@@ -331,7 +332,7 @@
         VMEM((NY, 16, 256), bf16),
         VMEM((NX, 16, ROWS), bf16),
         VMEM((NX, 16, ROWS), bf16),
-        VMEM((NZ, NX, 16, ROWS), bf16),
+        VMEM((4, NZ, 4, 16, ROWS), bf16),
         VMEM((ROWS, FEATS), f32),
         DMA((4,)),
         DMA((3, NK)),
@@ -343,8 +344,7 @@
         DMA((2, NY)),
         DMA((2, NY)),
         DMA((2, NX)),
-        DMA((2, 16)),
-        DMA((2, 16)),
+        DMA((2, 4 * NZ)),
     ]
     return pl.pallas_call(
         kernel,

time: 67.9 us -> 61.8 us (0.910)
  the two profiles are of different devices: /device:TPU:6 before, /device:TPU:1 now
where the time goes in v3:
time: 61.8 us; the launch traced here: 61.7 us
  Pallas kernels  60.1 us (97%)
  local copies, waits for them, and re-layouts  1.57 us (3%)
    pallas_call x1, Pallas kernels, per_device(): pl.pallas_call(kernel, out_shape=jax.ShapeDtypeStruct((ROWS, FEATS), bf16...  60.1 us
    unnamed x1, local copies, waits for them, and re-layouts  1.57 us

profile of v3, /device:TPU:1, one launch (start us, length us, event | category | flops | bytes accessed | tf_op | source)
XLA Modules:
  0.0 61.7 jit_solution(15190919946419280105)
XLA Ops:
  0.0 60.1 %shard_map.64 = bf16[128,512]{1,0:T(8,128)(2,1)} custom-call(bf16[128,4096]{1,0:T(8,128)(2,1)} %x_hbm.1, bf16[3,4096,256]{2,1,0:T(8,128)(2,1)} %bitcast.4, bf16[3,3,256]{2,1,0:T(4,128)(2,1)} %taps_hbm.1, f32[16,128]{1,0:T(8,128)} %bitcast.6, f32[1,256]{1,0:T(1,128)} %bitcast.7, bf16[8,16,16,512]{3,2,1,0:T(8,128)(2,1)} %bitcast.5), custom_call_target="tpu_custom_call" | custom-call | tf_op jit(solution)/shard_map/pallas_call | solution.py:349
  60.1 1.6 %copy.8 = bf16[128,512]{1,0:T(8,128)(2,1)} copy(bf16[128,512]{1,0:T(8,128)(2,1)} %shard_map.64) | data formatting | bytes 262144

commit v4 on v3

v4 whole, which is shorter than its diff:
```python
import functools

import jax
import jax.numpy as jnp
from jax import lax
from jax.experimental import pallas as pl
from jax.experimental.pallas import tpu as pltpu
from jax.sharding import PartitionSpec as P

MESH = pl.DeviceIdType.MESH
NX = 16
NY = 8
NZ = 8
ROWS = 128
CHAN = 256
MODEL = 4096
FEATS = 512
KCH = 1024
NK = MODEL // KCH
TOEP = 16512


def kernel(
    x_hbm, w_hbm, taps_hbm, filt_hbm, skip_hbm, o_hbm, out_ref,
    xb, wb, ob, taps_v, filt_v, skip_v,
    pacc, halo_s, halo_r, ext, query_t, direct_t,
    fs, fr, hs, hr, toep, perm1, perm2, lhs,
    xs, xr, ys, yr, acc, ys2, yr2, xs2, xr2, hid, oacc,
    in_sem, w_sem, o_sem, halo_sem, f_sem, h_sem, x_sem, y_sem, y2_sem, x2_sem, z_sem,
):
    f32, bf16 = jnp.float32, jnp.bfloat16
    ctx = lax.axis_index("ctx")
    z = lax.axis_index("tp")
    y, xc = ctx // NX, ctx % NX
    x, core = xc // 2, xc % 2
    nxt, prv = (ctx + 1) % (NX * NY), (ctx + NX * NY - 1) % (NX * NY)

    def chip(t):
        return 4 + (t + 1) // 2 * (1 - 2 * (t % 2))

    def rowpeer(e, dc):
        return (x + e) % 8 * 2 + (core + dc) % 2

    def row_loop(one):
        @pl.loop(0, 7)
        def _(t):
            one(chip(t), 0)
            one(chip(t), 1)

        one(0, 1)

    copies = [
        pltpu.make_async_copy(x_hbm, xb, in_sem.at[0]),
        pltpu.make_async_copy(taps_hbm, taps_v, in_sem.at[1]),
        pltpu.make_async_copy(filt_hbm, filt_v, in_sem.at[2]),
        pltpu.make_async_copy(skip_hbm, skip_v, in_sem.at[3]),
    ]

    def wcopy(j, c):
        at = pl.ds(c * KCH, KCH)
        return pltpu.make_async_copy(w_hbm.at[j, at], wb.at[j, at], w_sem.at[j, c])

    def ocopy(k):
        p = rowpeer(k // 2, k % 2)
        return pltpu.make_async_copy(o_hbm.at[:, p], ob.at[k // 4, :, k % 4], o_sem)

    copies[0].start()
    for j in (1, 2):
        for c in range(NK):
            wcopy(j, c).start()
    copies[2].start()
    copies[1].start()
    copies[3].start()

    barrier = pltpu.get_barrier_semaphore()

    def greet(c, t):
        pl.semaphore_signal(barrier, inc=1, device_id=(c, t), device_id_type=MESH)

    row_loop(lambda e, dc: greet(y * NX + rowpeer(e, dc), z))

    @pl.loop(1, 8)
    def _(o):
        greet((y + o) % NY * NX + xc, z)
        greet(ctx, (z + o) % NZ)

    greet(nxt, z)
    greet(prv, z)

    row = lax.broadcasted_iota(jnp.int32, (256, 256), 0)
    col = lax.broadcasted_iota(jnp.int32, (256, 256), 1)
    take = (row % 16 // 2 * 2 + row // 16 % 2) * 16 + row // 32 * 2 + row % 2
    perm1[...] = jnp.where(col == take, 1.0, 0.0).astype(bf16)
    row = lax.broadcasted_iota(jnp.int32, (128, 128), 0)
    col = lax.broadcasted_iota(jnp.int32, (128, 128), 1)
    perm2[...] = jnp.where(col == (row % 16 // 2) * 16 + row // 16 * 2 + row % 2, 1.0, 0.0).astype(bf16)
    pacc[...] = jnp.zeros_like(pacc)
    acc[...] = jnp.zeros_like(acc)
    for k in range(1, 8):
        lhs[: 16 * k, k * 256 : (k + 1) * 256] = jnp.zeros((16 * k, 256), bf16)
    toep[128 * 128 :, :] = jnp.zeros((128, 128), bf16)

    def send(src, dst, sems, c, t, k=1):
        return pltpu.make_async_remote_copy(
            src_ref=src, dst_ref=dst, send_sem=sems.at[0], recv_sem=sems.at[k],
            device_id=(c, t), device_id_type=MESH)

    def arrived(at, sems, k=1):
        send(at, at, sems, ctx, z, k).wait_recv()

    def left(at, sems):
        send(at, at, sems, ctx, z).wait_send()

    def row_exchange(src, dst, sems):
        def one(e, dc):
            p = rowpeer(e, dc)
            send(src.at[p], dst.at[xc], sems, y * NX + p, z).start()

        row_loop(one)

    def row_all(at):
        return at.at[pl.ds(0, NX - 1)]

    def col_exchange(src_of, dst, sems):
        @pl.loop(0, 7)
        def _(t):
            p = (y + chip(t)) % NY
            send(src_of(p), dst.at[y], sems, p * NX + xc, z).start()

    def col_all(at):
        return at.at[pl.ds(0, NY - 1)]

    copies[0].wait()

    def project(j, c):
        wcopy(j, c).wait()
        at = pl.ds(pl.multiple_of(c * KCH, KCH), KCH)
        pacc[j] += jnp.dot(xb[:, at], wb[j, at, :], preferred_element_type=f32)

    def projected(j):
        rounded = pacc[j].astype(bf16)
        ext[j, 8:, :] = rounded.astype(f32)
        halo_s[j] = rounded[ROWS - 8 :, :]

    kv, q = pl.ds(1, 2), pl.ds(0, 1)

    def short_conv(j):
        before = halo_r[j].astype(f32)
        ext[j, :8, :] = jnp.where(ctx == 0, jnp.zeros_like(before), before)
        taps = [taps_v[i].astype(f32)[j : j + 1, :] for i in range(3)]
        return (
            taps[0] * ext[j, 8:, :]
            + taps[1] * ext[j, 7 : 7 + ROWS, :]
            + taps[2] * ext[j, 6 : 6 + ROWS, :]
        )

    copies[2].wait()
    for f in range(NX):
        fs[f] = filt_v[f : f + 1, :]

    @pl.loop(0, 2 * NK)
    def _(i):
        project(1 + i // NK, i % NK)

    projected(1)
    projected(2)
    for c in range(NK):
        wcopy(0, c).start()
    pl.semaphore_wait(barrier, NX - 1 + NY - 1 + 2 + NZ - 1)
    send(halo_s.at[kv], halo_r.at[kv], halo_sem, nxt, z).start()

    row_exchange(fs, fr, f_sem)
    fr[xc] = fs[xc]
    copies[1].wait()
    copies[3].wait()
    arrived(halo_r.at[kv], halo_sem)
    keyed = short_conv(1)
    gated = keyed * short_conv(2)
    xs[...] = gated.T.astype(bf16).reshape(NX, 16, ROWS)
    row_exchange(xs, xr, x_sem)
    xr[xc] = xs[xc]

    arrived(row_all(fr), f_sem)
    hs[...] = fr[...].reshape(NX, ROWS)
    col_exchange(lambda p: hs, hr, h_sem)
    hr[y] = hs[...]

    @pl.loop(0, NK)
    def _(c):
        project(0, c)

    projected(0)
    send(halo_s.at[q], halo_r.at[q], halo_sem, nxt, z, 2).start()
    direct_t[...] = (skip_v[...] * gated).T

    arrived(row_all(xr), x_sem)
    ys[...] = jnp.dot(
        perm1[...], xr[...].reshape(256, ROWS), preferred_element_type=f32
    ).astype(bf16).reshape(NY, 2, 16, ROWS)
    col_exchange(lambda p: ys.at[p], yr, y_sem)
    yr[y] = ys[y]

    @pl.loop(0, NX)
    def _(k):
        ocopy(k).start()


    lane = lax.broadcasted_iota(jnp.int32, (128, 128), 1)
    sub = lax.broadcasted_iota(jnp.int32, (128, 128), 0)
    keep = lane >= sub

    arrived(col_all(hr), h_sem)

    def toeplitz(p, before):
        for j in range(16):
            line = hr[p, j : j + 1, :]
            now = pltpu.roll(jnp.broadcast_to(line, (128, 128)), 0, 1, stride=1, stride_axis=0)
            at = pl.multiple_of((127 - j) * 128 - p * 2048, 128)
            toep[pl.ds(at, 128), :] = jnp.where(keep, now, before).astype(bf16)
            before = now
        return before

    lax.fori_loop(0, NY, toeplitz, jnp.zeros((128, 128), f32))

    arrived(col_all(yr), y_sem)
    for k in range(8):
        for p in range(8 - k):
            for par in range(2):
                at = k * 256 + par * 128
                lhs[16 * (p + k) : 16 * (p + k + 1), at : at + 128] = yr[p, par]

    @pl.loop(0, 8)
    def _(i):
        right = []
        for k in range(8):
            r0 = pl.multiple_of(14464 - 2048 * k + 256 * i, 128)
            r1 = pl.multiple_of(14336 - 2048 * k + 256 * i, 128)
            right.append(jnp.concatenate([toep[pl.ds(r0, 256), :], toep[pl.ds(r1, 256), :]], axis=1))
        acc[8:, :] = acc[6 : 6 + 128, :] + jnp.dot(
            lhs[...], jnp.concatenate(right, axis=0), preferred_element_type=f32
        )

    ys2[...] = acc[8:, :].astype(bf16).reshape(NY, 16, 256)
    col_exchange(lambda p: ys2.at[p], yr2, y2_sem)
    yr2[y] = ys2[y]
    arrived(halo_r.at[q], halo_sem, 2)
    query_t[...] = short_conv(0).T
    pltpu.make_async_copy(ob, ob, o_sem).wait()
    left(halo_s, halo_sem)
    left(row_all(fs), f_sem)
    left(row_all(xs), x_sem)
    left(col_all(hr), h_sem)
    left(col_all(ys), y_sem)
    arrived(col_all(yr2), y2_sem)
    back = jnp.dot(
        perm2[...], yr2[...].reshape(128, 256), preferred_element_type=f32
    ).astype(bf16)
    for b in range(8):
        for par in range(2):
            xs2[2 * b + par] = back[16 * b : 16 * b + 16, 128 * par : 128 * par + 128]
    def give(e, dc):
        p = rowpeer(e, dc)
        there = (8 - e) % 8
        send(xs2.at[p], xr2.at[2 * there + dc], x2_sem, y * NX + p, z, 1 + there // 2).start()

    row_loop(give)
    xr2[0] = xs2[xc]

    def zsend(g, o_block, o_to, k=None):
        at = hid.at[g, (z + o_block) % NZ]
        send(at, at, z_sem, ctx, (z + o_to) % NZ, 1 + g if k is None else k).start()

    relayed = (0, 3, 1)

    def own(g):
        arrived(xr2.at[pl.ds(1, 3) if g == 0 else pl.ds(4 * g, 4)], x2_sem, 1 + g)
        for k in range(4):
            at = pl.ds(pl.multiple_of(rowpeer(2 * g + k // 2, k % 2) * 16, 16), 16)
            hid[g, z, k] = (query_t[at, :] * (xr2[4 * g + k].astype(f32) + direct_t[at, :])).astype(bf16)
        if g not in relayed:
            zsend(g, 0, 4)
            zsend(g, 0, 5)
        else:
            zsend(g, 0, 5, 5 + g)
        for o in (3, 6, 2, 7, 1):
            zsend(g, 0, o)

    def relay(g):
        arrived(hid.at[g, (z + 3) % NZ], z_sem, 5 + g)
        zsend(g, 3, 7)

    def out_part(g):
        arrived(hid.at[g, pl.ds(0, 6 if g in relayed else 7)], z_sem, 1 + g)
        return lax.dot_general(
            hid[g].reshape(NZ * 64, ROWS), ob[g].reshape(NZ * 64, FEATS),
            (((0,), (0,)), ((), ())), preferred_element_type=f32)

    own(0)
    own(3)
    own(1)
    relay(0)
    own(2)
    relay(3)
    relay(1)
    oacc[...] = out_part(0)
    oacc[...] += out_part(3)
    oacc[...] += out_part(1)
    left(col_all(ys2), y2_sem)
    left(row_all(xs2), x2_sem)
    out_ref[...] = (oacc[...] + out_part(2)).astype(bf16)
    for g in range(4):
        left(hid.at[g, pl.ds(0, 7)], z_sem)


def per_device(hidden_in, in_proj, short_taps, long_filters, skip_gain, out_proj):
    f32, bf16 = jnp.float32, jnp.bfloat16
    VMEM, DMA = pltpu.VMEM, pltpu.SemaphoreType.DMA
    scratch = [
        VMEM((ROWS, MODEL), bf16),
        VMEM((3, MODEL, CHAN), bf16),
        VMEM((4, NZ, 4, 16, FEATS), bf16),
        VMEM((3, 3, CHAN), bf16),
        VMEM((NX, ROWS), f32),
        VMEM((1, CHAN), f32),
        VMEM((3, ROWS, CHAN), f32),
        VMEM((3, 8, CHAN), bf16),
        VMEM((3, 8, CHAN), bf16),
        VMEM((3, ROWS + 8, CHAN), f32),
        VMEM((CHAN, ROWS), f32),
        VMEM((CHAN, ROWS), f32),
        VMEM((NX, 1, ROWS), f32),
        VMEM((NX, 1, ROWS), f32),
        VMEM((NX, ROWS), f32),
        VMEM((NY, NX, ROWS), f32),
        VMEM((TOEP, 128), bf16),
        VMEM((256, 256), bf16),
        VMEM((128, 128), bf16),
        VMEM((128, 2048), bf16),
        VMEM((NX, 16, ROWS), bf16),
        VMEM((NX, 16, ROWS), bf16),
        VMEM((NY, 2, 16, ROWS), bf16),
        VMEM((NY, 2, 16, ROWS), bf16),
        VMEM((136, 256), f32),
        VMEM((NY, 16, 256), bf16),
        VMEM((NY, 16, 256), bf16),
        VMEM((NX, 16, ROWS), bf16),
        VMEM((NX, 16, ROWS), bf16),
        VMEM((4, NZ, 4, 16, ROWS), bf16),
        VMEM((ROWS, FEATS), f32),
        DMA((4,)),
        DMA((3, NK)),
        DMA,
        DMA((3,)),
        DMA((2,)),
        DMA((2,)),
        DMA((2,)),
        DMA((2,)),
        DMA((2,)),
        DMA((5,)),
        DMA((9,)),
    ]
    return pl.pallas_call(
        kernel,
        out_shape=jax.ShapeDtypeStruct((ROWS, FEATS), bf16),
        in_specs=[pl.BlockSpec(memory_space=pl.ANY)] * 6,
        out_specs=pl.BlockSpec(memory_space=pltpu.VMEM),
        scratch_shapes=scratch,
        compiler_params=pltpu.CompilerParams(
            collective_id=0, has_side_effects=True, vmem_limit_bytes=67043328
        ),
    )(
        hidden_in,
        jnp.transpose(in_proj, (1, 0, 2)),
        short_taps,
        long_filters.T,
        skip_gain.reshape(1, CHAN),
        out_proj.reshape(NZ, NX, 16, FEATS),
    )


def solution(mesh):
    in_specs = (
        P("ctx", None),
        P(None, None, "tp"),
        P(None, None, "tp"),
        P("ctx", "tp"),
        P("tp"),
        P(None, "tp"),
    )
    return jax.shard_map(
        per_device, mesh=mesh, in_specs=in_specs, out_specs=P("ctx", "tp"), check_vma=False
    )
```

time: 61.8 us -> 59.6 us (0.964)
  Pallas kernels: 60.1 us -> 57.9 us
    pallas_call x1, Pallas kernels: 60.1 us -> 57.9 us  [per_device(): pl.pallas_call(kernel, out_shape=jax.ShapeDtypeStruct((ROWS, FEATS), bf16...]
where the time goes in v4:
time: 59.6 us; the launch traced here: 59.5 us
  Pallas kernels  57.9 us (97%)
  local copies, waits for them, and re-layouts  1.57 us (3%)
    pallas_call x1, Pallas kernels, per_device(): pl.pallas_call(kernel, out_shape=jax.ShapeDtypeStruct((ROWS, FEATS), bf16...  57.9 us
    unnamed x1, local copies, waits for them, and re-layouts  1.57 us

profile of v4, /device:TPU:1, one launch (start us, length us, event | category | flops | bytes accessed | tf_op | source)
XLA Modules:
  0.0 59.5 jit_solution(6246811853466677782)
XLA Ops:
  0.0 57.9 %shard_map.64 = bf16[128,512]{1,0:T(8,128)(2,1)} custom-call(bf16[128,4096]{1,0:T(8,128)(2,1)} %x_hbm.1, bf16[3,4096,256]{2,1,0:T(8,128)(2,1)} %bitcast.4, bf16[3,3,256]{2,1,0:T(4,128)(2,1)} %taps_hbm.1, f32[16,128]{1,0:T(8,128)} %bitcast.6, f32[1,256]{1,0:T(1,128)} %bitcast.7, bf16[8,16,16,512]{3,2,1,0:T(8,128)(2,1)} %bitcast.5), custom_call_target="tpu_custom_call" | custom-call | tf_op jit(solution)/shard_map/pallas_call | solution.py:362
  57.9 1.6 %copy.8 = bf16[128,512]{1,0:T(8,128)(2,1)} copy(bf16[128,512]{1,0:T(8,128)(2,1)} %shard_map.64) | data formatting | bytes 262144

commit v5 on v4

--- a/solution.py
+++ b/solution.py
@@ -64,11 +64,11 @@
         p = rowpeer(k // 2, k % 2)
         return pltpu.make_async_copy(o_hbm.at[:, p], ob.at[k // 4, :, k % 4], o_sem)
 
+    copies[2].start()
     copies[0].start()
     for j in (1, 2):
         for c in range(NK):
             wcopy(j, c).start()
-    copies[2].start()
     copies[1].start()
     copies[3].start()
 
@@ -130,6 +130,13 @@
     def col_all(at):
         return at.at[pl.ds(0, NY - 1)]
 
+    copies[2].wait()
+    for f in range(NX):
+        fs[f] = filt_v[f : f + 1, :]
+    pl.semaphore_wait(barrier, NX - 1 + NY - 1 + 2 + NZ - 1)
+    row_exchange(fs, fr, f_sem)
+    fr[xc] = fs[xc]
+
     copies[0].wait()
 
     def project(j, c):
@@ -154,9 +161,6 @@
             + taps[2] * ext[j, 6 : 6 + ROWS, :]
         )
 
-    copies[2].wait()
-    for f in range(NX):
-        fs[f] = filt_v[f : f + 1, :]
 
     @pl.loop(0, 2 * NK)
     def _(i):
@@ -166,11 +170,8 @@
     projected(2)
     for c in range(NK):
         wcopy(0, c).start()
-    pl.semaphore_wait(barrier, NX - 1 + NY - 1 + 2 + NZ - 1)
     send(halo_s.at[kv], halo_r.at[kv], halo_sem, nxt, z).start()
 
-    row_exchange(fs, fr, f_sem)
-    fr[xc] = fs[xc]
     copies[1].wait()
     copies[3].wait()
     arrived(halo_r.at[kv], halo_sem)

time: 59.6 us -> 61.7 us (1.035)
  Pallas kernels: 57.9 us -> 60 us
    pallas_call x1, Pallas kernels: 57.9 us -> 60 us  [per_device(): pl.pallas_call(kernel, out_shape=jax.ShapeDtypeStruct((ROWS, FEATS), bf16...]
where the time goes in v5:
time: 61.7 us; the launch traced here: 61.5 us
  Pallas kernels  60 us (97%)
  local copies, waits for them, and re-layouts  1.57 us (3%)
    pallas_call x1, Pallas kernels, per_device(): pl.pallas_call(kernel, out_shape=jax.ShapeDtypeStruct((ROWS, FEATS), bf16...  60 us
    unnamed x1, local copies, waits for them, and re-layouts  1.57 us

profile of v5, /device:TPU:1, one launch (start us, length us, event | category | flops | bytes accessed | tf_op | source)
XLA Modules:
  0.0 61.5 jit_solution(15999046271293423724)
XLA Ops:
  0.0 60.0 %shard_map.64 = bf16[128,512]{1,0:T(8,128)(2,1)} custom-call(bf16[128,4096]{1,0:T(8,128)(2,1)} %x_hbm.1, bf16[3,4096,256]{2,1,0:T(8,128)(2,1)} %bitcast.4, bf16[3,3,256]{2,1,0:T(4,128)(2,1)} %taps_hbm.1, f32[16,128]{1,0:T(8,128)} %bitcast.6, f32[1,256]{1,0:T(1,128)} %bitcast.7, bf16[8,16,16,512]{3,2,1,0:T(8,128)(2,1)} %bitcast.5), custom_call_target="tpu_custom_call" | custom-call | tf_op jit(solution)/shard_map/pallas_call | solution.py:363
  60.0 1.6 %copy.8 = bf16[128,512]{1,0:T(8,128)(2,1)} copy(bf16[128,512]{1,0:T(8,128)(2,1)} %shard_map.64) | data formatting | bytes 262144

commit v6 on v4

--- a/solution.py
+++ b/solution.py
@@ -26,7 +26,7 @@
     pacc, halo_s, halo_r, ext, query_t, direct_t,
     fs, fr, hs, hr, toep, perm1, perm2, lhs,
     xs, xr, ys, yr, acc, ys2, yr2, xs2, xr2, hid, oacc,
-    in_sem, w_sem, o_sem, halo_sem, f_sem, h_sem, x_sem, y_sem, y2_sem, x2_sem, z_sem,
+    in_sem, xi_sem, w_sem, o_sem, halo_sem, f_sem, h_sem, x_sem, y_sem, y2_sem, x2_sem, z_sem,
 ):
     f32, bf16 = jnp.float32, jnp.bfloat16
     ctx = lax.axis_index("ctx")
@@ -50,11 +50,14 @@
         one(0, 1)
 
     copies = [
-        pltpu.make_async_copy(x_hbm, xb, in_sem.at[0]),
-        pltpu.make_async_copy(taps_hbm, taps_v, in_sem.at[1]),
-        pltpu.make_async_copy(filt_hbm, filt_v, in_sem.at[2]),
-        pltpu.make_async_copy(skip_hbm, skip_v, in_sem.at[3]),
+        pltpu.make_async_copy(taps_hbm, taps_v, in_sem.at[0]),
+        pltpu.make_async_copy(filt_hbm, filt_v, in_sem.at[1]),
+        pltpu.make_async_copy(skip_hbm, skip_v, in_sem.at[2]),
     ]
+
+    def xcopy(c):
+        at = pl.ds(c * KCH, KCH)
+        return pltpu.make_async_copy(x_hbm.at[:, at], xb.at[:, at], xi_sem.at[c])
 
     def wcopy(j, c):
         at = pl.ds(c * KCH, KCH)
@@ -64,13 +67,12 @@
         p = rowpeer(k // 2, k % 2)
         return pltpu.make_async_copy(o_hbm.at[:, p], ob.at[k // 4, :, k % 4], o_sem)
 
-    copies[0].start()
-    for j in (1, 2):
-        for c in range(NK):
-            wcopy(j, c).start()
-    copies[2].start()
-    copies[1].start()
-    copies[3].start()
+    for c in range(NK):
+        xcopy(c).start()
+        wcopy(1, c).start()
+        wcopy(2, c).start()
+    for copy in copies:
+        copy.start()
 
     barrier = pltpu.get_barrier_semaphore()
 
@@ -130,12 +132,6 @@
     def col_all(at):
         return at.at[pl.ds(0, NY - 1)]
 
-    copies[0].wait()
-
-    def project(j, c):
-        wcopy(j, c).wait()
-        at = pl.ds(pl.multiple_of(c * KCH, KCH), KCH)
-        pacc[j] += jnp.dot(xb[:, at], wb[j, at, :], preferred_element_type=f32)
 
     def projected(j):
         rounded = pacc[j].astype(bf16)
@@ -154,13 +150,20 @@
             + taps[2] * ext[j, 6 : 6 + ROWS, :]
         )
 
-    copies[2].wait()
+    copies[1].wait()
     for f in range(NX):
         fs[f] = filt_v[f : f + 1, :]
 
-    @pl.loop(0, 2 * NK)
-    def _(i):
-        project(1 + i // NK, i % NK)
+    @pl.loop(0, NK)
+    def _(c):
+        for copy in (xcopy(c), wcopy(1, c), wcopy(2, c)):
+            copy.wait()
+        at = pl.ds(pl.multiple_of(c * KCH, KCH), KCH)
+        both = jnp.dot(
+            xb[:, at], jnp.concatenate([wb[1, at, :], wb[2, at, :]], axis=1), preferred_element_type=f32
+        )
+        pacc[1] += both[:, :CHAN]
+        pacc[2] += both[:, CHAN:]
 
     projected(1)
     projected(2)
@@ -171,8 +174,8 @@
 
     row_exchange(fs, fr, f_sem)
     fr[xc] = fs[xc]
-    copies[1].wait()
-    copies[3].wait()
+    copies[0].wait()
+    copies[2].wait()
     arrived(halo_r.at[kv], halo_sem)
     keyed = short_conv(1)
     gated = keyed * short_conv(2)
@@ -187,7 +190,9 @@
 
     @pl.loop(0, NK)
     def _(c):
-        project(0, c)
+        wcopy(0, c).wait()
+        at = pl.ds(pl.multiple_of(c * KCH, KCH), KCH)
+        pacc[0] += jnp.dot(xb[:, at], wb[0, at, :], preferred_element_type=f32)
 
     projected(0)
     send(halo_s.at[q], halo_r.at[q], halo_sem, nxt, z, 2).start()
@@ -347,7 +352,8 @@
         VMEM((NX, 16, ROWS), bf16),
         VMEM((4, NZ, 4, 16, ROWS), bf16),
         VMEM((ROWS, FEATS), f32),
-        DMA((4,)),
+        DMA((3,)),
+        DMA((NK,)),
         DMA((3, NK)),
         DMA,
         DMA((3,)),

time: 59.6 us -> 59.9 us (level)
  no operation moved by 1% of the time
where the time goes in v6:
time: 59.9 us; the launch traced here: 59.7 us
  Pallas kernels  58.2 us (97%)
  local copies, waits for them, and re-layouts  1.57 us (3%)
    pallas_call x1, Pallas kernels, per_device(): pl.pallas_call(kernel, out_shape=jax.ShapeDtypeStruct((ROWS, FEATS), bf16...  58.2 us
    unnamed x1, local copies, waits for them, and re-layouts  1.57 us

profile of v6, /device:TPU:1, one launch (start us, length us, event | category | flops | bytes accessed | tf_op | source)
XLA Modules:
  0.0 59.7 jit_solution(15982782303257756641)
XLA Ops:
  0.0 58.2 %shard_map.64 = bf16[128,512]{1,0:T(8,128)(2,1)} custom-call(bf16[128,4096]{1,0:T(8,128)(2,1)} %x_hbm.1, bf16[3,4096,256]{2,1,0:T(8,128)(2,1)} %bitcast.4, bf16[3,3,256]{2,1,0:T(4,128)(2,1)} %taps_hbm.1, f32[16,128]{1,0:T(8,128)} %bitcast.6, f32[1,256]{1,0:T(1,128)} %bitcast.7, bf16[8,16,16,512]{3,2,1,0:T(8,128)(2,1)} %bitcast.5), custom_call_target="tpu_custom_call" | custom-call | tf_op jit(solution)/shard_map/pallas_call | solution.py:368
  58.2 1.6 %copy.8 = bf16[128,512]{1,0:T(8,128)(2,1)} copy(bf16[128,512]{1,0:T(8,128)(2,1)} %shard_map.64) | data formatting | bytes 262144

commit v7 on v6

--- a/solution.py
+++ b/solution.py
@@ -234,16 +234,15 @@
                 at = k * 256 + par * 128
                 lhs[16 * (p + k) : 16 * (p + k + 1), at : at + 128] = yr[p, par]
 
-    @pl.loop(0, 8)
+    @pl.loop(0, 4)
     def _(i):
         right = []
         for k in range(8):
-            r0 = pl.multiple_of(14464 - 2048 * k + 256 * i, 128)
-            r1 = pl.multiple_of(14336 - 2048 * k + 256 * i, 128)
-            right.append(jnp.concatenate([toep[pl.ds(r0, 256), :], toep[pl.ds(r1, 256), :]], axis=1))
-        acc[8:, :] = acc[6 : 6 + 128, :] + jnp.dot(
-            lhs[...], jnp.concatenate(right, axis=0), preferred_element_type=f32
-        )
+            at = [pl.multiple_of(14464 - 2048 * k + 512 * i + r, 128) for r in (0, -128, 256, 128)]
+            right.append(jnp.concatenate([toep[pl.ds(r, 256), :] for r in at], axis=1))
+        both = jnp.dot(lhs[...], jnp.concatenate(right, axis=0), preferred_element_type=f32)
+        acc[8:, :] = acc[6 : 6 + 128, :] + both[:, :256]
+        acc[8:, :] = acc[6 : 6 + 128, :] + both[:, 256:]
 
     ys2[...] = acc[8:, :].astype(bf16).reshape(NY, 16, 256)
     col_exchange(lambda p: ys2.at[p], yr2, y2_sem)
@@ -300,13 +299,10 @@
             hid[g].reshape(NZ * 64, ROWS), ob[g].reshape(NZ * 64, FEATS),
             (((0,), (0,)), ((), ())), preferred_element_type=f32)
 
-    own(0)
-    own(3)
-    own(1)
-    relay(0)
-    own(2)
-    relay(3)
-    relay(1)
+    for g in (0, 3, 1, 2):
+        own(g)
+    for g in relayed:
+        relay(g)
     oacc[...] = out_part(0)
     oacc[...] += out_part(3)
     oacc[...] += out_part(1)

time: 59.9 us -> 59.1 us (0.987)
  Pallas kernels: 58.2 us -> 57.4 us
    pallas_call x1, Pallas kernels: 58.2 us -> 57.4 us  [per_device(): pl.pallas_call(kernel, out_shape=jax.ShapeDtypeStruct((ROWS, FEATS), bf16...]
where the time goes in v7:
time: 59.1 us; the launch traced here: 59 us
  Pallas kernels  57.4 us (97%)
  local copies, waits for them, and re-layouts  1.57 us (3%)
    pallas_call x1, Pallas kernels, per_device(): pl.pallas_call(kernel, out_shape=jax.ShapeDtypeStruct((ROWS, FEATS), bf16...  57.4 us
    unnamed x1, local copies, waits for them, and re-layouts  1.57 us

profile of v7, /device:TPU:1, one launch (start us, length us, event | category | flops | bytes accessed | tf_op | source)
XLA Modules:
  0.0 59.0 jit_solution(3042555348950238946)
XLA Ops:
  0.0 57.4 %shard_map.64 = bf16[128,512]{1,0:T(8,128)(2,1)} custom-call(bf16[128,4096]{1,0:T(8,128)(2,1)} %x_hbm.1, bf16[3,4096,256]{2,1,0:T(8,128)(2,1)} %bitcast.4, bf16[3,3,256]{2,1,0:T(4,128)(2,1)} %taps_hbm.1, f32[16,128]{1,0:T(8,128)} %bitcast.6, f32[1,256]{1,0:T(1,128)} %bitcast.7, bf16[8,16,16,512]{3,2,1,0:T(8,128)(2,1)} %bitcast.5), custom_call_target="tpu_custom_call" | custom-call | tf_op jit(solution)/shard_map/pallas_call | solution.py:364
  57.4 1.6 %copy.8 = bf16[128,512]{1,0:T(8,128)(2,1)} copy(bf16[128,512]{1,0:T(8,128)(2,1)} %shard_map.64) | data formatting | bytes 262144

commit v8 on v7

--- a/solution.py
+++ b/solution.py
@@ -188,14 +188,6 @@
     col_exchange(lambda p: hs, hr, h_sem)
     hr[y] = hs[...]
 
-    @pl.loop(0, NK)
-    def _(c):
-        wcopy(0, c).wait()
-        at = pl.ds(pl.multiple_of(c * KCH, KCH), KCH)
-        pacc[0] += jnp.dot(xb[:, at], wb[0, at, :], preferred_element_type=f32)
-
-    projected(0)
-    send(halo_s.at[q], halo_r.at[q], halo_sem, nxt, z, 2).start()
     direct_t[...] = (skip_v[...] * gated).T
 
     arrived(row_all(xr), x_sem)
@@ -247,10 +239,15 @@
     ys2[...] = acc[8:, :].astype(bf16).reshape(NY, 16, 256)
     col_exchange(lambda p: ys2.at[p], yr2, y2_sem)
     yr2[y] = ys2[y]
-    arrived(halo_r.at[q], halo_sem, 2)
-    query_t[...] = short_conv(0).T
+    @pl.loop(0, NK)
+    def _(c):
+        wcopy(0, c).wait()
+        at = pl.ds(pl.multiple_of(c * KCH, KCH), KCH)
+        pacc[0] += jnp.dot(xb[:, at], wb[0, at, :], preferred_element_type=f32)
+
+    projected(0)
+    send(halo_s.at[q], halo_r.at[q], halo_sem, nxt, z, 2).start()
     pltpu.make_async_copy(ob, ob, o_sem).wait()
-    left(halo_s, halo_sem)
     left(row_all(fs), f_sem)
     left(row_all(xs), x_sem)
     left(col_all(hr), h_sem)
@@ -269,6 +266,9 @@
 
     row_loop(give)
     xr2[0] = xs2[xc]
+    arrived(halo_r.at[q], halo_sem, 2)
+    query_t[...] = short_conv(0).T
+    left(halo_s, halo_sem)
 
     def zsend(g, o_block, o_to, k=None):
         at = hid.at[g, (z + o_block) % NZ]

time: 59.1 us -> 59.1 us (level)
  no operation moved by 1% of the time
where the time goes in v8:
time: 59.1 us; the launch traced here: 59 us
  Pallas kernels  57.4 us (97%)
  local copies, waits for them, and re-layouts  1.57 us (3%)
    pallas_call x1, Pallas kernels, per_device(): pl.pallas_call(kernel, out_shape=jax.ShapeDtypeStruct((ROWS, FEATS), bf16...  57.4 us
    unnamed x1, local copies, waits for them, and re-layouts  1.57 us

profile of v8, /device:TPU:1, one launch (start us, length us, event | category | flops | bytes accessed | tf_op | source)
XLA Modules:
  0.0 59.0 jit_solution(7354251724991110133)
XLA Ops:
  0.0 57.4 %shard_map.64 = bf16[128,512]{1,0:T(8,128)(2,1)} custom-call(bf16[128,4096]{1,0:T(8,128)(2,1)} %x_hbm.1, bf16[3,4096,256]{2,1,0:T(8,128)(2,1)} %bitcast.4, bf16[3,3,256]{2,1,0:T(4,128)(2,1)} %taps_hbm.1, f32[16,128]{1,0:T(8,128)} %bitcast.6, f32[1,256]{1,0:T(1,128)} %bitcast.7, bf16[8,16,16,512]{3,2,1,0:T(8,128)(2,1)} %bitcast.5), custom_call_target="tpu_custom_call" | custom-call | tf_op jit(solution)/shard_map/pallas_call | solution.py:364
  57.4 1.6 %copy.8 = bf16[128,512]{1,0:T(8,128)(2,1)} copy(bf16[128,512]{1,0:T(8,128)(2,1)} %shard_map.64) | data formatting | bytes 262144
